TPU v7x, 32 devices: a whole 2x2x4 slice. The times are simulated.
32 devices in a mesh: row: 8 (over y, x, core), col: 4 (over z).
Axes of the slice: x: 2, y: 2, z: 4, core: 2. Of those that a mesh axis runs over, the one named last changes fastest.
Arguments:
- classes: int32 [128, 64], P('row', 'col'), may hold values from 0 to 15
- features: bfloat16 [128, 64, 128], P('row', 'col'), may hold values from -6 to 6
- cotangent: bfloat16 [128, 64, 128], P('row', 'col'), may hold values from -6 to 6
- table: float32 [16, 128], replicated, may hold values from -6 to 6
- norm_gain: float32 [128], replicated, may hold values from 0.5 to 1.5
- in_weight: bfloat16 [128, 512], replicated, may hold values from -0.5 to 0.5
- scan_weight: bfloat16 [256, 160], replicated, may hold values from -0.375 to 0.375
- step_weight: float32 [4, 8, 256], replicated, may hold values from -2 to 2
- step_bias: float32 [4, 256], replicated, may hold values from -6 to -2.5
- decay_log: float32 [4, 16, 256], replicated, may hold values from -4 to 2
- skip_gain: float32 [4, 256], replicated, may hold values from 0.5 to 1.5
- output_gain: float32 [256], replicated, may hold values from 0.5 to 1.5
- output_weight: bfloat16 [256, 128], replicated, may hold values from -0.375 to 0.375
Outputs:
- feature_grad: bfloat16 [128, 64, 128], P('row', 'col')
- in_weight_grad: float32 [128, 512], replicated
- scan_weight_grad: float32 [256, 160], replicated
- step_weight_grad: float32 [4, 8, 256], replicated
- step_bias_grad: float32 [4, 256], replicated
- decay_log_grad: float32 [4, 16, 256], replicated
- skip_gain_grad: float32 [4, 256], replicated
- norm_gain_grad: float32 [128], replicated
- output_gain_grad: float32 [256], replicated
- output_weight_grad: float32 [256, 128], replicated
All inputs are finite; a program needn't handle non-finite values.
Results may differ from a plain program's by a relative error of at most 0.0076.
Values sent between devices are 32-bit elements; how exact they have to be, the bound alone decides.
A program may use at most 320 MiB of HBM per device.

v0:
```python
import functools
import math

import jax
import jax.numpy as jnp
from jax import lax
from jax.experimental import pallas as pl
from jax.experimental.pallas import tpu as pltpu
from jax.sharding import PartitionSpec as P

EPS = 1e-05
HIGHEST = lax.Precision.HIGHEST
MESH = pl.DeviceIdType.MESH
LANES = 128
SUB = 8
LOG2E = math.log2(math.e)
VMEM = pl.BlockSpec(memory_space=pltpu.VMEM)
BIG = 60 * 1024 * 1024


def layer_norm(rows, gain):
    average = jnp.mean(rows, axis=-1, keepdims=True)
    centred = rows - average
    spread = jnp.mean(centred * centred, axis=-1, keepdims=True)
    return centred * lax.rsqrt(spread + EPS) * gain


def silu_slope(before):
    sigma = jax.nn.sigmoid(before)
    return sigma * (1.0 + before * (1.0 - sigma))


def embed(features, classes, table):
    labels = jnp.arange(table.shape[0], dtype=jnp.int32)
    onehot = (classes[..., None] == labels).astype(jnp.float32)
    lookup = jnp.einsum("hwk,kd->hwd", onehot, table, precision=HIGHEST)
    return features.astype(jnp.float32) + lookup


def gate_output(total, gate_in, output_gain):
    return layer_norm(total, output_gain) * jax.nn.silu(gate_in)


def greet(axes):
    barrier = pltpu.get_barrier_semaphore()
    partners = 0
    for axis in axes:
        count = lax.axis_size(axis)
        me = lax.axis_index(axis)
        for d in range(1, count):
            pl.semaphore_signal(
                barrier, inc=1, device_id={axis: lax.rem(me + d, count)}, device_id_type=MESH
            )
            partners += 1
    pl.semaphore_wait(barrier, partners)


def half(ref, k, h, t):
    return ref[k, h, pl.ds(t, 1), :]


def walk(lines, tile, blocks, group, start, step):
    def outer(b, carry):
        def inner(j, carry):
            time = b * tile + j
            rising = b * (tile * lines) + j
            falling = (blocks - 1 - b) * (tile * lines) + (tile - 1 - j)
            tokens = [[base + line * tile for line in group] for base in (rising, falling)]
            return step(carry, tokens, time)

        return lax.fori_loop(0, tile, inner, carry, unroll=2)

    return lax.fori_loop(0, blocks, outer, start)


def groups_of(lines):
    size = 2 if lines % 2 == 0 else 1
    return [tuple(range(g, g + size)) for g in range(0, lines, size)]


def fold(ref, k, h, count):
    total = ref[k, h, pl.ds(0, count, stride=SUB), :]
    for s in range(1, SUB):
        total = total + ref[k, h, pl.ds(s, count, stride=SUB), :]
    return total


def softplus(x):
    return jnp.maximum(x, 0.0) + jnp.log1p(jnp.exp(-jnp.abs(x)))


def cross(a, b):
    return lax.dot_general(a, b, (((0,), (0,)), ((), ())), preferred_element_type=jnp.float32)


def back(a, b):
    return lax.dot_general(a, b, (((1,), (1,)), ((), ())), preferred_element_type=jnp.float32)


def block_kernel(
    tile_rows, tile_cols, states, rank, grad_scale, tiles,
    embedded_ref, upstream_ref, norm_gain_ref, in_weight_ref, scan_weight_ref, step_weight_ref,
    step_bias_ref, rate_ref, skip_ref, output_gain_ref, output_weight_ref,
    feature_ref, in_grad_ref, scan_grad_ref, stepw_ref, stepb_ref, dr_ref, skip_grad_ref,
    norm_grad_ref, gain_grad_ref, out_grad_ref,
    mixed, gate_grad, turn, along, down, wide, sv, steps, slope, low, hist, eight, pace8, up, dproj, dr_acc,
    mine0, from0, side0, all0, mine1, from1, side1, all1, sems, sumsems,
):
    count, inner = tile_rows * tile_cols, output_weight_ref.shape[0]
    rows, cols = lax.axis_size("row"), lax.axis_size("col")
    eh, nh = inner // LANES, states // SUB
    group = rank + 2 * states
    shapes = ((tile_rows // cols, tile_cols), (tile_cols // rows, tile_rows))
    boxes = (along, down)
    axes = ("col", "row")
    greet(("row", "col"))

    def post(turn_number, pair):
        axis, box = axes[pair], boxes[pair]
        size = lax.axis_size(axis)
        me = lax.axis_index(axis)
        copies = []
        for d in range(1, size):
            target = lax.rem(me + d, size)
            copy = pltpu.make_async_remote_copy(
                src_ref=box.at[2 * turn_number, target],
                dst_ref=box.at[2 * turn_number + 1, me],
                send_sem=sems.at[turn_number, pair, 0, d],
                recv_sem=sems.at[turn_number, pair, 1, d],
                device_id={axis: target},
                device_id_type=MESH,
            )
            copy.start()
            copies.append(copy)
        box[2 * turn_number + 1, me] = box[2 * turn_number, me]
        return copies

    def finish(copies):
        for copy in copies:
            copy.wait()

    def put_home(turn_number, x):
        along[2 * turn_number] = x.reshape(along.shape[1:])
        first = post(turn_number, 0)
        for h in range(eh):
            turn[h] = x[:, h * LANES : (h + 1) * LANES]
        per = tile_cols // rows
        for c in range(tile_cols):
            for h in range(eh):
                down[
                    2 * turn_number, c // per,
                    (c % per) * tile_rows : (c % per + 1) * tile_rows,
                    h * LANES : (h + 1) * LANES,
                ] = turn[h, pl.ds(c, tile_rows, stride=tile_cols), :]
        return first, post(turn_number, 1)

    def take_home(turn_number):
        per = tile_cols // rows
        for c in range(tile_cols):
            for h in range(eh):
                turn[h, pl.ds(c, tile_rows, stride=tile_cols), :] = down[
                    2 * turn_number + 1, c // per,
                    (c % per) * tile_rows : (c % per + 1) * tile_rows,
                    h * LANES : (h + 1) * LANES,
                ]
        here = along[2 * turn_number + 1].reshape(count, inner)
        return here + jnp.concatenate([turn[h] for h in range(eh)], axis=1)

    def lines_in(turn_number, pair):
        return boxes[pair][2 * turn_number + 1].reshape(count, inner)

    def lines_out(turn_number, pair, x):
        boxes[pair][2 * turn_number] = x.reshape(boxes[pair].shape[1:])
        return post(turn_number, pair)

    def rate_of(d, m, h):
        return rate_ref[d, m * SUB : (m + 1) * SUB, h * LANES : (h + 1) * LANES]

    def part(h):
        return slice(h * LANES, (h + 1) * LANES)

    zero = jnp.zeros((SUB, LANES), jnp.float32)

    sums = ((mine0, from0, side0, all0), (mine1, from1, side1, all1))
    fill = [0, 0]

    def put(lot, x):
        mine = sums[lot][0]
        per = mine.shape[1] // SUB
        for i in range(x.shape[0] // SUB):
            tile = fill[lot]
            at = (tile % per) * SUB
            mine[tile // per, at : at + SUB, :] = x[i * SUB : (i + 1) * SUB]
            fill[lot] += 1

    def put_wide(lot, x):
        for h in range(x.shape[1] // LANES):
            put(lot, x[:, h * LANES : (h + 1) * LANES])

    taken = [0, 0]

    def take(lot, height):
        full = sums[lot][3]
        per = full.shape[1] // SUB
        out = []
        for i in range(height // SUB):
            tile = taken[lot]
            at = (tile % per) * SUB
            out.append(full[tile // per, at : at + SUB, :])
            taken[lot] += 1
        return jnp.concatenate(out, axis=0) * grad_scale

    def take_wide(lot, height, width):
        return jnp.concatenate([take(lot, height) for h in range(width // LANES)], axis=1)

    def pad_rows(*rows_in):
        missing = -len(rows_in) % SUB
        return jnp.concatenate(list(rows_in) + [jnp.zeros((missing, LANES), jnp.float32)], axis=0)

    def pad_lot(lot):
        while fill[lot] < tiles[lot]:
            put(lot, zero)

    def spread(lot, phase, axis, source, result):
        size = lax.axis_size(axis)
        me = lax.axis_index(axis)
        copies = []
        for d in range(1, size):
            target = lax.rem(me + d, size)
            copy = pltpu.make_async_remote_copy(
                src_ref=source(target),
                dst_ref=result(me, d),
                send_sem=sumsems.at[lot, phase, 0, d],
                recv_sem=sumsems.at[lot, phase, 1, d],
                device_id={axis: target},
                device_id_type=MESH,
            )
            copy.start()
            copies.append(copy)
        return copies

    def sum_scatter(lot):
        mine, other, side, full = sums[lot]
        pad_lot(lot)
        return spread(lot, 0, "row", lambda t: mine.at[t], lambda me, d: other.at[d - 1])

    def sum_across(lot, copies):
        mine, other, side, full = sums[lot]
        finish(copies)
        acc = mine[lax.axis_index("row")]
        for d in range(rows - 1):
            acc = acc + other[d]
        me = lax.axis_index("col")
        side[me] = acc
        return spread(lot, 1, "col", lambda t: side.at[me], lambda m, d: side.at[m])

    def sum_gather(lot, copies):
        mine, other, side, full = sums[lot]
        finish(copies)
        acc = side[0]
        for d in range(1, cols):
            acc = acc + side[d]
        me = lax.axis_index("row")
        full[me] = acc
        return spread(lot, 2, "row", lambda t: full.at[me], lambda m, d: full.at[m])

    embedded = embedded_ref[...]
    normed = layer_norm(embedded, norm_gain_ref[...]).astype(jnp.bfloat16)
    mixed[...] = jnp.dot(normed, in_weight_ref[...], preferred_element_type=jnp.float32)
    values = jax.nn.silu(mixed[:, :inner]).astype(jnp.bfloat16).astype(jnp.float32)
    arriving = put_home(0, values)

    leaving = []
    for pair in range(2):
        lines, tile = shapes[pair]
        length = count // lines
        blocks = length // tile
        finish(arriving[pair])
        value = lines_in(0, pair)
        wide_p, sv_p, steps_p, hist_p = wide.at[pair], sv.at[pair], steps.at[pair], hist.at[pair]
        weight = scan_weight_ref[:, 2 * pair * group : 2 * (pair + 1) * group]
        projected = jnp.dot(
            value.astype(jnp.bfloat16), weight, preferred_element_type=jnp.float32
        )
        for k in range(2):
            d = 2 * pair + k
            lowrank = projected[:, k * group : k * group + rank]
            low[d] = lowrank
            before = (
                jnp.dot(
                    lowrank, step_weight_ref[d], precision=HIGHEST,
                    preferred_element_type=jnp.float32,
                )
                + step_bias_ref[d : d + 1, :]
            )
            slope[d] = jax.nn.sigmoid(before)
            pace = softplus(before)
            for h in range(eh):
                steps_p[k, h] = pace[:, part(h)]
                sv_p[k, h] = pace[:, part(h)] * value[:, part(h)]
            for which in range(2):
                for n in range(states):
                    col = k * group + rank + which * states + n
                    wide_p[k, which, pl.ds(n, count, stride=states), :] = jnp.broadcast_to(
                        projected[:, col : col + 1], (count, LANES)
                    )
            for h in range(eh):
                for line in range(lines):
                    at = line * (length + 1) * states
                    hist_p[k, h, at : at + states, :] = jnp.zeros((states, LANES), jnp.float32)
        for lot in groups_of(lines):

            def advance(carry, tokens, time):
                new = []
                i = 0
                for k in range(2):
                    for line, t in zip(lot, tokens[k]):
                        drive = [half(sv_p, k, h, t) for h in range(eh)]
                        pace = [half(steps_p, k, h, t) for h in range(eh)]
                        sums = [None] * eh
                        for m in range(nh):
                            at = pl.ds(pl.multiple_of(t * states + m * SUB, SUB), SUB)
                            slot = (line * (length + 1) + time + 1) * states + m * SUB
                            source = wide_p[k, 0, at, :]
                            probe = wide_p[k, 1, at, :]
                            for h in range(eh):
                                a = jnp.exp2(pace[h] * rate_of(2 * pair + k, m, h))
                                state = a * carry[i] + source * drive[h]
                                i += 1
                                hist_p[k, h, pl.ds(pl.multiple_of(slot, SUB), SUB), :] = state
                                new.append(state)
                                term = probe * state
                                sums[h] = term if sums[h] is None else sums[h] + term
                        for h in range(eh):
                            eight[k, h, pl.ds(pl.multiple_of(t * SUB, SUB), SUB), :] = sums[h]
                return tuple(new)

            walk(lines, tile, blocks, lot, (zero,) * (2 * len(lot) * eh * nh), advance)
        skip = skip_ref[2 * pair : 2 * pair + 1, :] + skip_ref[2 * pair + 1 : 2 * pair + 2, :]
        y = skip * value + jnp.concatenate(
            [fold(eight, 0, h, count) + fold(eight, 1, h, count) for h in range(eh)], axis=1
        )
        leaving.append(lines_out(1, pair, y))
    finish(leaving[0])
    finish(leaving[1])
    total = take_home(1)

    upstream = upstream_ref[...]
    gated, gate_pull = jax.vjp(gate_output, total, mixed[:, inner:], output_gain_ref[...])
    d_gated = back(upstream, output_weight_ref[...])
    d_total, d_gate_in, gain_grad = gate_pull(d_gated)
    arriving = put_home(2, d_total)
    gate_grad[...] = d_gate_in
    put(0, pad_rows(*[gain_grad[:, part(h)] for h in range(eh)]))
    put_wide(0, cross(gated.astype(jnp.bfloat16), upstream))

    leaving = []
    for pair in range(2):
        lines, tile = shapes[pair]
        length = count // lines
        blocks = length // tile
        finish(arriving[pair])
        g_all = lines_in(2, pair)
        wide_p, sv_p, steps_p, hist_p = wide.at[pair], sv.at[pair], steps.at[pair], hist.at[pair]
        for h in range(eh):
            up[0, h] = g_all[:, part(h)]
        for lot in groups_of(lines):

            def retreat(carry, tokens, time):
                grads, rates = carry
                rates = list(rates)
                new = []
                i = 0
                for k in range(2):
                    for line, t in zip(lot, tokens[1 - k]):
                        drive = [half(sv_p, k, h, t) for h in range(eh)]
                        pace = [half(steps_p, k, h, t) for h in range(eh)]
                        g = [half(up, 0, h, t) for h in range(eh)]
                        dd = [None] * eh
                        dp = [None] * eh
                        for m in range(nh):
                            at = pl.ds(pl.multiple_of(t * states + m * SUB, SUB), SUB)
                            slot = (line * (length + 1) + length - 1 - time) * states + m * SUB
                            earlier = pl.ds(pl.multiple_of(slot, SUB), SUB)
                            current = pl.ds(pl.multiple_of(slot + states, SUB), SUB)
                            source = wide_p[k, 0, at, :]
                            probe = wide_p[k, 1, at, :]
                            flow = None
                            read = None
                            for h in range(eh):
                                rate = rate_of(2 * pair + k, m, h)
                                grad = grads[i] + probe * g[h]
                                i += 1
                                term = grad * drive[h]
                                flow = term if flow is None else flow + term
                                term = g[h] * hist_p[k, h, current, :]
                                read = term if read is None else read + term
                                term = grad * source
                                dd[h] = term if dd[h] is None else dd[h] + term
                                carried = jnp.exp2(pace[h] * rate) * grad
                                q = carried * hist_p[k, h, earlier, :]
                                term = q * rate
                                dp[h] = term if dp[h] is None else dp[h] + term
                                j = (k * nh + m) * eh + h
                                rates[j] = rates[j] + q * pace[h]
                                new.append(carried)
                            wide_p[k, 0, at, :] = flow
                            wide_p[k, 1, at, :] = read
                        for h in range(eh):
                            at8 = pl.ds(pl.multiple_of(t * SUB, SUB), SUB)
                            eight[k, h, at8, :] = dd[h]
                            pace8[k, h, at8, :] = dp[h]
                return (tuple(new), tuple(rates))

            chains = 2 * len(lot) * eh * nh
            unused, rates = walk(
                lines, tile, blocks, lot, ((zero,) * chains, (zero,) * (2 * eh * nh)), retreat
            )
            for k in range(2):
                for m in range(nh):
                    for h in range(eh):
                        place = (2 * pair + k, slice(m * SUB, (m + 1) * SUB), part(h))
                        add = rates[(k * nh + m) * eh + h] * rate_ref[place] * (1.0 / LOG2E)
                        if lot[0] == 0:
                            dr_acc[place] = add
                        else:
                            dr_acc[place] += add
        value = lines_in(0, pair)
        g_all = lines_in(2, pair)
        skip = skip_ref[2 * pair : 2 * pair + 1, :] + skip_ref[2 * pair + 1 : 2 * pair + 2, :]
        dv = skip * g_all
        direct = jnp.sum(g_all * value, axis=0, keepdims=True)
        small = [direct[:, part(h)] for h in range(eh)]
        for k in range(2):
            d = 2 * pair + k
            drive = jnp.concatenate([fold(eight, k, h, count) for h in range(eh)], axis=1)
            pace = jnp.concatenate([fold(pace8, k, h, count) for h in range(eh)], axis=1)
            dv = dv + drive * jnp.concatenate([steps_p[k, h] for h in range(eh)], axis=1)
            d_before = (drive * value + pace * (1.0 / LOG2E)) * slope[d]
            bias_sum = jnp.sum(d_before, axis=0, keepdims=True)
            small += [bias_sum[:, part(h)] for h in range(eh)]
            put_wide(
                pair,
                lax.dot_general(
                    low[d], d_before, (((0,), (0,)), ((), ())), precision=HIGHEST,
                    preferred_element_type=jnp.float32,
                ),
            )
            put_wide(pair, dr_acc[d])
            dproj[:, k * group : k * group + rank] = lax.dot_general(
                d_before, step_weight_ref[d], (((1,), (1,)), ((), ())), precision=HIGHEST,
                preferred_element_type=jnp.float32,
            )
            lane = lax.broadcasted_iota(jnp.int32, (LANES, 2 * states), 1)
            flow = None
            for j in range(2 * states):
                x = wide_p[k, j // states, pl.ds(j % states, count, stride=states), :]
                pick = (lane == j).astype(jnp.bfloat16)
                term = jnp.dot(x.astype(jnp.bfloat16), pick, preferred_element_type=jnp.float32)
                flow = term if flow is None else flow + term
            dproj[:, k * group + rank : (k + 1) * group] = flow
        d_projected = dproj[...].astype(jnp.bfloat16)
        span = slice(2 * pair * group, 2 * (pair + 1) * group)
        leaving.append(lines_out(3, pair, back(d_projected, scan_weight_ref[:, span]) + dv))
        put(pair, pad_rows(*small))
        put_wide(pair, cross(d_projected, value.astype(jnp.bfloat16)))
        if pair == 0:
            early = sum_scatter(0)
        else:
            early = sum_across(0, early)
    finish(leaving[0])
    finish(leaving[1])
    d_values = take_home(3)
    early = sum_gather(0, early)

    d_mixed = jnp.concatenate(
        [d_values * silu_slope(mixed[:, :inner]), gate_grad[...]], axis=1
    ).astype(jnp.bfloat16)
    normed, norm_pull = jax.vjp(layer_norm, embedded_ref[...], norm_gain_ref[...])
    put_wide(1, cross(normed.astype(jnp.bfloat16), d_mixed))
    d_embedded, norm_grad = norm_pull(back(d_mixed, in_weight_ref[...]))
    put(1, pad_rows(norm_grad))
    late = sum_scatter(1)
    feature_ref[...] = (upstream_ref[...].astype(jnp.float32) + d_embedded).astype(jnp.bfloat16)
    late = sum_across(1, late)
    finish(early)
    late = sum_gather(1, late)

    def take_pair(pair):
        for d in (2 * pair, 2 * pair + 1):
            stepw_ref[d] = take_wide(pair, rank, inner)
            dr_ref[d] = take_wide(pair, states, inner)
        small = take(pair, -(-3 * eh // SUB) * SUB)
        for h in range(eh):
            for k in range(2):
                d = 2 * pair + k
                skip_grad_ref[d : d + 1, part(h)] = small[h : h + 1]
                stepb_ref[d : d + 1, part(h)] = small[(k + 1) * eh + h : (k + 1) * eh + h + 1]
        span = slice(2 * pair * group, 2 * (pair + 1) * group)
        scan_grad_ref[:, span] = take_wide(pair, 2 * group, inner).T

    small = take(0, SUB)
    for h in range(eh):
        gain_grad_ref[:, part(h)] = small[h : h + 1]
    out_grad_ref[...] = take_wide(0, inner, out_grad_ref.shape[1])
    take_pair(0)
    finish(late)
    take_pair(1)
    in_grad_ref[...] = take_wide(1, in_grad_ref.shape[0], in_grad_ref.shape[1])
    norm_grad_ref[...] = take(1, SUB)[0:1]


def local(
    classes, features, cotangent, table, norm_gain, in_weight, scan_weight, step_weight,
    step_bias, decay_log, skip_gain, output_gain, output_weight,
):
    tile_rows, tile_cols, model_width = features.shape
    inner = output_weight.shape[0]
    count = tile_rows * tile_cols
    rows, cols = lax.axis_size("row"), lax.axis_size("col")
    rank = step_weight.shape[1]
    states = decay_log.shape[1]
    group = rank + 2 * states
    eh = inner // LANES
    lines = max(tile_rows // cols, tile_cols // rows)
    grad_scale = float(count * rows * cols) ** (-0.5)
    rate2 = -jnp.exp(decay_log) * LOG2E
    embedded = embed(features, classes, table).reshape(count, model_width)
    f32 = jnp.float32
    shapes = [
        ((count, model_width), jnp.bfloat16),
        (in_weight.shape, f32),
        (scan_weight.shape, f32),
        (step_weight.shape, f32),
        (step_bias.shape, f32),
        (decay_log.shape, f32),
        (skip_gain.shape, f32),
        ((1, model_width), f32),
        ((1, inner), f32),
        (output_weight.shape, f32),
    ]
    scratch = [
        ((count, 2 * inner), f32),
        ((count, inner), f32),
        ((eh, count, LANES), f32),
        ((8, cols, count // cols, inner), f32),
        ((8, rows, count // rows, inner), f32),
        ((2, 2, 2, count * states, LANES), f32),
        ((2, 2, eh, count, LANES), f32),
        ((2, 2, eh, count, LANES), f32),
        ((4, count, inner), f32),
        ((4, count, rank), f32),
        ((2, 2, eh, (count + lines) * states, LANES), f32),
        ((2, eh, count * SUB, LANES), f32),
        ((2, eh, count * SUB, LANES), f32),
        ((1, eh, count, LANES), f32),
        ((count, 2 * group), f32),
        (decay_log.shape, f32),
    ]
    pair_tiles = eh * (2 * rank + 2 * states + 2 * group) // SUB + -(-3 * eh // SUB)
    least = (
        1 + inner * model_width // (LANES * SUB) + pair_tiles,
        1 + in_weight.size // (LANES * SUB) + pair_tiles,
    )
    tiles = tuple(-(-t // rows) * rows for t in least)
    for lot in range(2):
        chunk = (tiles[lot] // rows * SUB, LANES)
        scratch += [((rows,) + chunk, f32), ((rows - 1,) + chunk, f32), ((cols,) + chunk, f32), ((rows,) + chunk, f32)]
    feature_grad, *grads = pl.pallas_call(
        functools.partial(block_kernel, tile_rows, tile_cols, states, rank, grad_scale, tiles),
        out_shape=[jax.ShapeDtypeStruct(*s) for s in shapes],
        in_specs=[VMEM] * 11,
        out_specs=[VMEM] * 10,
        scratch_shapes=[pltpu.VMEM(*s) for s in scratch]
        + [
            pltpu.SemaphoreType.DMA((4, 2, 2, max(rows, cols))),
            pltpu.SemaphoreType.DMA((2, 3, 2, max(rows, cols))),
        ],
        compiler_params=pltpu.CompilerParams(
            vmem_limit_bytes=BIG, collective_id=1, has_side_effects=True
        ),
    )(
        embedded, cotangent.reshape(count, model_width), norm_gain[None], in_weight, scan_weight,
        step_weight, step_bias, rate2, skip_gain, output_gain[None], output_weight,
    )
    feature_grad = feature_grad.reshape(tile_rows, tile_cols, model_width)
    grads[6], grads[7] = grads[6][0], grads[7][0]
    return (feature_grad, *grads)


def solution(mesh):
    in_specs = (P("row", "col"), P("row", "col", None), P("row", "col", None)) + (P(),) * 10
    out_specs = (P("row", "col", None),) + (P(),) * 9
    return jax.shard_map(local, mesh=mesh, in_specs=in_specs, out_specs=out_specs, check_vma=False)
```

profile of v0, /device:TPU:0, one launch (start us, length us, event | category | flops | bytes accessed | tf_op | source)
XLA Modules:
  0.0 99.3 jit_solution(17494533834338341345)
XLA Ops:
  0.6 0.0 copy-start
  0.7 0.0 copy-start.4
  0.7 0.0 copy-start.8
  0.7 1.5 %negate_multiply_fusion.rate_ref = f32[4,16,256]{2,1,0:T(8,128)} fusion(f32[4,16,256]{2,1,0:T(8,128)} %param.22), kind=kLoop, calls=%fused_computation.2 | loop fusion | flops 32768 | bytes 131072 | tf_op jit(solution)/shard_map/mul | solution.py:527
  2.2 0.0 copy-done
  2.2 0.0 copy-done.4
  2.2 0.0 copy-done.8
  2.2 0.0 copy-start.3
  2.2 0.9 convolution_add_fusion
  3.1 0.0 copy-done.3
  3.1 0.8 copy.23.scan_weight_ref
  3.9 87.8 %shard_map.204 = (bf16[256,128]{1,0:T(8,128)(2,1)}, f32[128,512]{1,0:T(8,128)}, f32[256,160]{1,0:T(8,128)}, f32[4,8,256]{2,1,0:T(8,128)}, f32[4,256]{1,0:T(4,128...) custom-call(f32[256,128]{1,0:T(8,128)} %bitcast.10, ...), custom_call_target="tpu_custom_call" | custom-call | tf_op jit(solution)/shard_map/pallas_call | solution.py:569
  91.7 0.0 copy-start.6
  91.7 0.0 copy-start.1
  91.7 1.8 %copy.24 = f32[256,160]{0,1:T(8,128)} copy(f32[256,160]{1,0:T(8,128)} %get-tuple-element.32) | data formatting | bytes 327680
  93.5 0.0 copy-done.6
  93.5 0.6 copy.34
  94.1 0.0 copy-done.1
  94.1 0.7 copy.35
  94.8 0.0 copy-done.7
  94.9 0.6 copy.36
  95.5 0.0 copy-done.10
  95.5 0.6 copy.37
  96.1 0.6 copy.38
  96.7 0.0 copy-done.9
  96.7 0.6 copy.39
  97.3 0.1 copy-done.12
  97.4 0.5 copy.40
  97.9 0.1 copy-done.11
  98.1 0.6 copy.41
  98.6 0.0 copy-done.2
  98.6 0.7 copy.42
  (8 shorter events, 0.0 us)
Async XLA Ops:
  0.6 1.6 %copy-start = (f32[16,128]{1,0:T(8,128)S(1)}, f32[16,128]{1,0:T(8,128)}, u32[]{:S(2)}) copy-start(f32[16,128]{1,0:T(8,128)} %param.16) | copy-start | bytes 24580
  0.7 1.5 %copy-start.4 = (bf16[16,16,128]{2,1,0:T(8,128)(2,1)S(1)}, bf16[16,16,128]{2,1,0:T(8,128)(2,1)}, u32[]{:S(2)}) copy-start(bf16[16,16,128]{2,1,0:T(8,128)(2,1)} %param.14) | copy-start | bytes 196612
  0.7 1.5 %copy-start.8 = (s32[16,16]{1,0:T(8,128)S(1)}, s32[16,16]{1,0:T(8,128)}, u32[]{:S(2)}) copy-start(s32[16,16]{1,0:T(8,128)} %param.13) | copy-start | bytes 3076
  2.2 0.9 copy-start.3
  91.7 1.8 %copy-start.6 = (bf16[256,128]{1,0:T(8,128)(2,1)S(1)}, bf16[256,128]{1,0:T(8,128)(2,1)}, u32[]{:S(2)}) copy-start(bf16[256,128]{1,0:T(8,128)(2,1)} %get-tuple-element.20) | copy-start | bytes 196612
  91.7 2.4 %copy-start.1 = (f32[128,512]{1,0:T(8,128)S(1)}, f32[128,512]{1,0:T(8,128)}, u32[]{:S(2)}) copy-start(f32[128,512]{1,0:T(8,128)} %get-tuple-element.51) | copy-start | bytes 786436
  94.1 0.8 copy-start.7
  94.1 1.4 %copy-start.10 = (f32[4,256]{1,0:T(4,128)S(1)}, f32[4,256]{1,0:T(4,128)}, u32[]{:S(2)}) copy-start(f32[4,256]{1,0:T(4,128)} %get-tuple-element.54) | copy-start | bytes 12292
  94.1 2.0 %copy-start.5 = (f32[4,16,256]{2,1,0:T(8,128)S(1)}, f32[4,16,256]{2,1,0:T(8,128)}, u32[]{:S(2)}) copy-start(f32[4,16,256]{2,1,0:T(8,128)} %get-tuple-element.55) | copy-start | bytes 196612
  94.9 3.8 %copy-start.2 = (f32[256,128]{1,0:T(8,128)S(1)}, f32[256,128]{1,0:T(8,128)}, u32[]{:S(2)}) copy-start(f32[256,128]{1,0:T(8,128)} %get-tuple-element.59) | copy-start | bytes 393220
  96.1 0.7 copy-start.9
  96.7 0.7 copy-start.12
  97.4 0.7 copy-start.11
where the time goes:
time: 99.6 us; the launch traced here: 99.3 us
  Pallas kernels  87.8 us (88%)
  local copies, waits for them, and re-layouts  8.37 us (8%)
  other arithmetic  1.52 us (2%)
    pallas_call x1, Pallas kernels, local(): pl.pallas_call(functools.partial(block_kernel, tile_rows, tile_cols, stat...  87.8 us
    unnamed x37, local copies, waits for them, and re-layouts  8.37 us

commit v1 on v0

--- a/solution.py
+++ b/solution.py
@@ -97,7 +97,7 @@
     return lax.dot_general(a, b, (((1,), (1,)), ((), ())), preferred_element_type=jnp.float32)
 
 
-def block_kernel(
+def general_kernel(
     tile_rows, tile_cols, states, rank, grad_scale, tiles,
     embedded_ref, upstream_ref, norm_gain_ref, in_weight_ref, scan_weight_ref, step_weight_ref,
     step_bias_ref, rate_ref, skip_ref, output_gain_ref, output_weight_ref,
@@ -510,7 +510,7 @@
     norm_grad_ref[...] = take(1, SUB)[0:1]
 
 
-def local(
+def general(
     classes, features, cotangent, table, norm_gain, in_weight, scan_weight, step_weight,
     step_bias, decay_log, skip_gain, output_gain, output_weight,
 ):
@@ -567,7 +567,7 @@
         chunk = (tiles[lot] // rows * SUB, LANES)
         scratch += [((rows,) + chunk, f32), ((rows - 1,) + chunk, f32), ((cols,) + chunk, f32), ((rows,) + chunk, f32)]
     feature_grad, *grads = pl.pallas_call(
-        functools.partial(block_kernel, tile_rows, tile_cols, states, rank, grad_scale, tiles),
+        functools.partial(general_kernel, tile_rows, tile_cols, states, rank, grad_scale, tiles),
         out_shape=[jax.ShapeDtypeStruct(*s) for s in shapes],
         in_specs=[VMEM] * 11,
         out_specs=[VMEM] * 10,
@@ -588,6 +588,803 @@
     return (feature_grad, *grads)
 
 
+def split2(x):
+    high = x.astype(jnp.bfloat16)
+    return high, (x - high.astype(jnp.float32)).astype(jnp.bfloat16)
+
+
+def dot(a, b):
+    return jnp.dot(a, b, preferred_element_type=jnp.float32)
+
+
+def greet_all():
+    barrier = pltpu.get_barrier_semaphore()
+    rows, cols = lax.axis_size("row"), lax.axis_size("col")
+    r, c = lax.axis_index("row"), lax.axis_index("col")
+    for dr in range(rows):
+        for dc in range(cols):
+            if dr or dc:
+                there = {"row": lax.rem(r + dr, rows), "col": lax.rem(c + dc, cols)}
+                pl.semaphore_signal(barrier, inc=1, device_id=there, device_id_type=MESH)
+    pl.semaphore_wait(barrier, rows * cols - 1)
+
+
+def lots_of(rows, inner, model_width, states, rank, group, eh):
+    small = -(-5 * eh // SUB) * SUB
+    pair = 2 * (rank + states) * eh + small + 2 * group * eh
+    early = inner * model_width // LANES + model_width * eh + SUB + pair
+    late = model_width * eh + SUB + pair
+    per = SUB * rows
+    return tuple(-(-n // per) * per for n in (early, late))
+
+
+def fast_kernel(
+    tile_rows, tile_cols, states, rank,
+    embedded_ref, upstream_ref, norm_gain_ref, in_weight_ref, sw_ref, step_weight_ref,
+    step_bias_ref, decay_ref, skip_ref, output_gain_ref, output_weight_ref,
+    feature_ref, early_ref, late_ref,
+    home, emb_s0, emb_s1, emb_r0, emb_r1, cot_s0, cot_s1, cot_r0, cot_r1,
+    back_s0, back_s1, back_r0, back_r1, y_s0, y_s1, y_r0, y_r1,
+    spread0, spread1, wpk, swp, cmat, rate_s, normed_s, mixed_s, value_s, proj_s, tok, slope,
+    wide, hist, pace_t, drive_t, bufs, bufs_tok, probe_t, lhs, dval, dr_s, in_acc, norm_acc,
+    mine0, from0, side0, mine1, from1, side1, sems, ysems, sumsems,
+):
+    f32, bf16 = jnp.float32, jnp.bfloat16
+    count, inner = tile_rows * tile_cols, output_weight_ref.shape[0]
+    model = embedded_ref.shape[1]
+    rows, cols = lax.axis_size("row"), lax.axis_size("col")
+    me_r, me_c = lax.axis_index("row"), lax.axis_index("col")
+    eh = inner // LANES
+    group = rank + 2 * states
+    lines = (tile_rows // cols, tile_cols // rows)
+    length = (count // lines[0], count // lines[1])
+    copies_m = tuple(SUB // (2 * n) for n in lines)
+    per_n = tuple(states // m for m in copies_m)
+    tall = tuple(SUB * n for n in length)
+    blocks = count // SUB
+    axes = ("col", "row")
+    sizes = (cols, rows)
+    zero = jnp.zeros((SUB, LANES), f32)
+    sub = lax.broadcasted_iota(jnp.int32, (SUB, LANES), 0)
+    even = lax.rem(sub, 2) == 0
+    pos = sub // 2
+    pos_even = lax.rem(pos, 2) == 0
+    pos_edge = (pos == 0) | (pos == 3)
+    low_half = sub < 4
+
+    def part(h):
+        return slice(h * LANES, (h + 1) * LANES)
+
+    def tile(b):
+        return pl.ds(pl.multiple_of(b * SUB, SUB), SUB)
+
+    greet_all()
+
+    def pack(src, dst, p):
+        if p == 0:
+            for rho in range(tile_rows):
+                c, i = rho // lines[0], rho % lines[0]
+                for j in range(2):
+                    dst[c, pl.ds(2 * i + j, tile_cols // 2, stride=SUB), :] = src[
+                        pl.ds(rho * tile_cols + j, tile_cols // 2, stride=2), :
+                    ]
+        else:
+            for r in range(rows):
+                for j in range(2):
+                    dst[r, pl.ds(j, tile_rows, stride=2), :] = src[
+                        pl.ds(2 * r + j, tile_rows, stride=tile_cols), :
+                    ]
+
+    def unpack(src, dst, p):
+        if p == 0:
+            for rho in range(tile_rows):
+                c, i = rho // lines[0], rho % lines[0]
+                for j in range(2):
+                    dst[pl.ds(rho * tile_cols + j, tile_cols // 2, stride=2), :] = src[
+                        c, pl.ds(2 * i + j, tile_cols // 2, stride=SUB), :
+                    ]
+        else:
+            for r in range(rows):
+                for j in range(2):
+                    dst[pl.ds(2 * r + j, tile_rows, stride=tile_cols), :] = src[
+                        r, pl.ds(j, tile_rows, stride=2), :
+                    ]
+
+    def exchange(turn, p, src, dst):
+        size, axis = sizes[p], axes[p]
+        me = lax.axis_index(axis)
+        out = []
+        for d in range(1, size):
+            target = lax.rem(me + d, size)
+            copy = pltpu.make_async_remote_copy(
+                src_ref=src.at[target],
+                dst_ref=dst.at[me],
+                send_sem=sems.at[turn, p, 0, d],
+                recv_sem=sems.at[turn, p, 1, d],
+                device_id={axis: target},
+                device_id_type=MESH,
+            )
+            copy.start()
+            out.append(copy)
+        dst[me] = src[me]
+        return out
+
+    def swap(p, src, dst):
+        out = []
+        for dr in range(rows):
+            for dc in range(cols):
+                r, c = lax.rem(me_r + dr, rows), lax.rem(me_c + dc, cols)
+                if p == 0:
+                    there, here = c * rows + r, me_r * cols + me_c
+                else:
+                    there, here = r * cols + c, me_c * rows + me_r
+                if dr == 0 and dc == 0:
+                    dst[here] = src[there]
+                    continue
+                copy = pltpu.make_async_remote_copy(
+                    src_ref=src.at[there],
+                    dst_ref=dst.at[here],
+                    send_sem=ysems.at[p, 0, dr * cols + dc],
+                    recv_sem=ysems.at[p, 1, dr * cols + dc],
+                    device_id={"row": r, "col": c},
+                    device_id_type=MESH,
+                )
+                copy.start()
+                out.append(copy)
+        return out
+
+    def arrived(copies):
+        for copy in copies:
+            copy.wait_recv()
+
+    def sent(copies):
+        for copy in copies:
+            copy.wait_send()
+
+    emb_s, emb_r = (emb_s0, emb_s1), (emb_r0, emb_r1)
+    cot_s, cot_r = (cot_s0, cot_s1), (cot_r0, cot_r1)
+    back_s, back_r = (back_s0, back_s1), (back_r0, back_r1)
+    y_s, y_r = (y_s0, y_s1), (y_r0, y_r1)
+    spreads = (spread0, spread1)
+    pending = []
+
+    pack(embedded_ref, emb_s1, 1)
+    emb1 = exchange(0, 1, emb_s1, emb_r1)
+    pack(embedded_ref, emb_s0, 0)
+    emb0 = exchange(0, 0, emb_s0, emb_r0)
+    home[...] = upstream_ref[...].astype(f32)
+    pack(home, cot_s0, 0)
+    cot0 = exchange(1, 0, cot_s0, cot_r0)
+    pack(home, cot_s1, 1)
+    cot1 = exchange(1, 1, cot_s1, cot_r1)
+    pending += emb1 + emb0 + cot0 + cot1
+
+    key_row = lax.broadcasted_iota(jnp.int32, (LANES, 2 * LANES), 0)
+    lane_tile = lax.broadcasted_iota(jnp.int32, (LANES, 2 * LANES), 1) // LANES
+    for p in range(2):
+        which = lax.rem(key_row, 2 * states) // states
+        key = which * per_n[p] + lax.rem(key_row, per_n[p])
+        key = jnp.where(key_row < 4 * states, key - lane_tile, -8 * states)
+        for q in range(per_n[p]):
+            spreads[p][:, 2 * q * LANES : 2 * (q + 1) * LANES] = jnp.where(
+                key == 2 * q, 1.0, 0.0
+            ).astype(bf16)
+    sw32 = sw_ref[...].astype(f32)
+    for d in range(4):
+        off = d * group
+        low_w = sw32[off : off + rank]
+        wpk[d] = jnp.concatenate(
+            [sw32[off + rank : off + group], low_w,
+             jnp.zeros((LANES - group, inner), f32)], axis=0
+        ).astype(bf16)
+        step_w = step_weight_ref[d]
+        w1, w2 = split2(step_w)
+        w3 = (step_w - w1.astype(f32) - w2.astype(f32)).astype(bf16)
+        blank = jnp.zeros((rank, inner), f32)
+        left = jnp.concatenate([low_w, low_w, low_w, blank], axis=0).astype(bf16)
+        right = jnp.concatenate(
+            [w1.astype(f32), w2.astype(f32), w3.astype(f32), blank], axis=0
+        ).astype(bf16)
+        c_high, c_low = split2(cross(left, right))
+        cmat[d, 0] = c_high
+        cmat[d, 1] = c_low
+        for i, w in enumerate((w1, w2)):
+            swp[d, i] = jnp.concatenate(
+                [jnp.zeros((2 * states, inner), f32), w.astype(f32),
+                 jnp.zeros((LANES - group, inner), f32)], axis=0
+            ).astype(bf16)
+        rate = -jnp.exp(decay_ref[d]) * LOG2E
+        p, k = d // 2, d % 2
+        for n in range(states):
+            m, n1 = n // per_n[p], n % per_n[p]
+            for h in range(eh):
+                row = jnp.broadcast_to(rate[n : n + 1, part(h)], (SUB, LANES))
+                if p == 0:
+                    mask = lax.rem(sub, 2) == k
+                else:
+                    mask = pos == 2 * m + k
+                at = slice(n1 * SUB, (n1 + 1) * SUB)
+                if k == 0 and m == 0:
+                    rate_s[p, h, at, :] = row
+                else:
+                    rate_s[p, h, at, :] = jnp.where(mask, row, rate_s[p, h, at, :])
+
+    def to_scan(p, first, second, store):
+        def one(b, carry):
+            mirror = blocks - 1 - b
+            x0, x1 = first(tile(b)), second(tile(mirror))
+            if p == 0:
+                z = jnp.where(even, x1, x0)
+                store(tile(2 * b), jnp.where(even, x0, x1))
+                store(
+                    tile(2 * b + 1),
+                    jnp.where(even, pltpu.roll(z, SUB - 1, 0), pltpu.roll(z, 1, 0)),
+                )
+            else:
+                u = jnp.where(pos_even, x0, x1)
+                v = pltpu.roll(u, 4, 0)
+                u2 = pltpu.roll(jnp.where(pos_even, x1, x0), 2, 0)
+                v2 = pltpu.roll(u2, 4, 0)
+                store(tile(4 * b), jnp.where(pos_edge, u, v))
+                store(tile(4 * b + 1), jnp.where(low_half, v2, u2))
+                store(tile(4 * b + 2), jnp.where(pos_edge, v, u))
+                store(tile(4 * b + 3), jnp.where(low_half, u2, v2))
+            return carry
+
+        lax.fori_loop(0, blocks, one, 0, unroll=4)
+
+    def from_scan(p, load, store):
+        def one(b, carry):
+            mirror = blocks - 1 - b
+            if p == 0:
+                s0, s1 = load(tile(2 * b)), load(tile(2 * b + 1))
+                store(0, tile(b), jnp.where(even, s0, pltpu.roll(s1, 1, 0)))
+                store(1, tile(mirror), jnp.where(even, pltpu.roll(s1, SUB - 1, 0), s0))
+            else:
+                a = []
+                for i in range(4):
+                    s = load(tile(4 * b + i))
+                    s = s + pltpu.roll(s, 4, 0)
+                    a.append(pltpu.roll(s, 2, 0) if i % 2 else s)
+                store(
+                    0, tile(b),
+                    jnp.where(low_half, jnp.where(pos == 0, a[0], a[1]), jnp.where(pos == 2, a[2], a[3])),
+                )
+                store(
+                    1, tile(mirror),
+                    jnp.where(low_half, jnp.where(pos == 0, a[3], a[2]), jnp.where(pos == 2, a[1], a[0])),
+                )
+            return carry
+
+        lax.fori_loop(0, blocks, one, 0, unroll=4)
+
+    def prologue(p):
+        embedded = emb_r[p][...].reshape(count, model)
+        normed = layer_norm(embedded, norm_gain_ref[...]).astype(bf16)
+        normed_s[p] = normed
+        mixed_s[p] = dot(normed, in_weight_ref[...])
+        value = jax.nn.silu(mixed_s[p, :, :inner]).astype(bf16)
+        value_s[p] = value
+        value32 = value.astype(f32)
+        for k in range(2):
+            d = 2 * p + k
+            proj_s[p, k] = back(value, wpk[d])
+            before = dot(value, cmat[d, 0]) + dot(value, cmat[d, 1]) + step_bias_ref[d : d + 1, :]
+            slope[p, k] = jax.nn.sigmoid(before)
+            pace = softplus(before)
+            for h in range(eh):
+                tok[p, k, h] = pace[:, part(h)]
+        for h in range(eh):
+            for k in range(2):
+                bufs[k, :count, :] = tok[p, k, h] * value32[:, part(h)]
+
+            def put_pace(at, x, h=h):
+                pace_t[p, h, at, :] = x
+
+            def put_drive(at, x, h=h):
+                drive_t[p, h, at, :] = x
+
+            to_scan(p, lambda at, h=h: tok[p, 0, h, at, :], lambda at, h=h: tok[p, 1, h, at, :], put_pace)
+            to_scan(p, lambda at: bufs[0, at, :], lambda at: bufs[1, at, :], put_drive)
+
+        def put_probe(at, x):
+            probe_t[at, :] = x
+
+        to_scan(p, lambda at: proj_s[p, 0, at, :], lambda at: proj_s[p, 1, at, :], put_probe)
+        size_of = tall[p]
+        x = jnp.where(keep_lanes(p, size_of), probe_t[:size_of, :], 0.0)
+        high = x.astype(bf16).astype(f32)
+        lhs[:size_of, :] = (high + pltpu.roll(x - high, 2 * states, 1)).astype(bf16)
+        chunk = count
+        for q in range(per_n[p]):
+            w, n1 = 2 * q // per_n[p], 2 * q % per_n[p]
+            for s in range(size_of // chunk):
+                out = dot(
+                    lhs[s * chunk : (s + 1) * chunk, :],
+                    spreads[p][:, 2 * q * LANES : 2 * (q + 1) * LANES],
+                )
+                for j in range(2):
+                    at = (n1 + j) * size_of + s * chunk
+                    wide[p, w, at : at + chunk, :] = out[:, part(j)]
+
+    def keep_lanes(p, height):
+        lane = lax.broadcasted_iota(jnp.int32, (height, LANES), 1)
+        keep = lane < 2 * states
+        if copies_m[p] > 1:
+            row = lax.broadcasted_iota(jnp.int32, (height, LANES), 0)
+            m = lax.rem(row, SUB) // (SUB // copies_m[p])
+            keep = keep & (lax.rem(lane, states) // per_n[p] == m)
+        return keep
+
+    def forward(p):
+        high, stride = tall[p], tall[p] + SUB
+        half_n = 8
+        for h in range(eh):
+            for n in range(per_n[p]):
+                hist[p, h, n * stride : n * stride + SUB, :] = zero
+        for g in range(per_n[p] // half_n):
+            ns = range(g * half_n, (g + 1) * half_n)
+            rates = [[rate_s[p, h, n * SUB : (n + 1) * SUB, :] for h in range(eh)] for n in ns]
+
+            def step(t, carry, g=g, ns=ns, rates=rates):
+                at = tile(t)
+                pace = [pace_t[p, h, at, :] for h in range(eh)]
+                drive = [drive_t[p, h, at, :] for h in range(eh)]
+                y = [bufs[h, at, :] if g else None for h in range(eh)]
+                new = []
+                for i, n in enumerate(ns):
+                    row = tile(n * (high // SUB) + t)
+                    slot = tile(n * (stride // SUB) + t + 1)
+                    source, probe = wide[p, 0, row, :], wide[p, 1, row, :]
+                    for h in range(eh):
+                        a = jnp.exp2(pace[h] * rates[i][h])
+                        state = a * carry[i * eh + h] + source * drive[h]
+                        hist[p, h, slot, :] = state
+                        new.append(state)
+                        term = probe * state
+                        y[h] = term if y[h] is None else y[h] + term
+                for h in range(eh):
+                    bufs[h, at, :] = y[h]
+                return tuple(new)
+
+            lax.fori_loop(0, length[p], step, (zero,) * (half_n * eh), unroll=2)
+        for h in range(eh):
+
+            def put_y(k, at, x, h=h):
+                bufs[2 + k, at, :] = x
+
+            from_scan(p, lambda at, h=h: bufs[h, at, :], put_y)
+            y_s[p][:, :, part(h)] = (bufs[2, :count, :] + bufs[3, :count, :]).reshape(blocks, SUB, LANES)
+
+    def gate(p):
+        value = value_s[p].astype(f32)
+        skips = jnp.sum(skip_ref[...], axis=0, keepdims=True)
+        total = (
+            y_s[p][...].reshape(count, inner) + y_r[p][...].reshape(count, inner) + skips * value
+        )
+        upstream = cot_r[p][...].reshape(count, model).astype(bf16)
+        d_gated = back(upstream, output_weight_ref[...])
+        gated, pull = jax.vjp(gate_output, total, mixed_s[p, :, inner:], output_gain_ref[...])
+        d_total, d_gate_in, gain_grad = pull(d_gated)
+        dval[p] = d_total
+        if p == 0:
+            put(0, pad_rows(*[gain_grad[:, part(h)] for h in range(eh)]))
+            put_wide(0, cross(gated.astype(bf16), upstream))
+            d_gate = d_gate_in.astype(bf16)
+            gate16 = d_gate
+            put_wide(0, cross(normed_s[p], d_gate))
+        else:
+            gate16 = None
+
+        for h in range(eh):
+
+            def put_g(at, x, h=h):
+                bufs[h, at, :] = x
+
+            to_scan(
+                p, lambda at, h=h: dval[p, at, part(h)], lambda at, h=h: dval[p, at, part(h)], put_g
+            )
+        return gate16
+
+    sums = ((mine0, from0, side0, early_ref), (mine1, from1, side1, late_ref))
+    fill = [0, 0]
+
+    def put(lot, x):
+        mine = sums[lot][0]
+        per = mine.shape[1] // SUB
+        for i in range(x.shape[0] // SUB):
+            n = fill[lot]
+            at = (n % per) * SUB
+            mine[n // per, at : at + SUB, :] = x[i * SUB : (i + 1) * SUB]
+            fill[lot] += 1
+
+    def put_wide(lot, x):
+        for h in range(x.shape[1] // LANES):
+            put(lot, x[:, h * LANES : (h + 1) * LANES])
+
+    def pad_rows(*rows_in):
+        missing = -len(rows_in) % SUB
+        return jnp.concatenate(list(rows_in) + [jnp.zeros((missing, LANES), f32)], axis=0)
+
+    def pad_lot(lot):
+        mine = sums[lot][0]
+        while fill[lot] < rows * mine.shape[1] // SUB:
+            put(lot, zero)
+
+    def spread(lot, phase, axis, source, result):
+        size = lax.axis_size(axis)
+        me = lax.axis_index(axis)
+        out = []
+        for d in range(1, size):
+            target = lax.rem(me + d, size)
+            copy = pltpu.make_async_remote_copy(
+                src_ref=source(target),
+                dst_ref=result(me, d),
+                send_sem=sumsems.at[lot, phase, 0, d],
+                recv_sem=sumsems.at[lot, phase, 1, d],
+                device_id={axis: target},
+                device_id_type=MESH,
+            )
+            copy.start()
+            out.append(copy)
+        pending.extend(out)
+        return out
+
+    def sum_scatter(lot):
+        mine, other, side, full = sums[lot]
+        pad_lot(lot)
+        return spread(lot, 0, "row", lambda t: mine.at[t], lambda me, d: other.at[d - 1])
+
+    def sum_across(lot, copies):
+        mine, other, side, full = sums[lot]
+        arrived(copies)
+        acc = mine[me_r]
+        for d in range(rows - 1):
+            acc = acc + other[d]
+        side[me_c] = acc
+        return spread(lot, 1, "col", lambda t: side.at[me_c], lambda m, d: side.at[m])
+
+    def sum_gather(lot, copies):
+        mine, other, side, full = sums[lot]
+        arrived(copies)
+        acc = side[0]
+        for d in range(1, cols):
+            acc = acc + side[d]
+        full[me_r] = acc
+        return spread(lot, 2, "row", lambda t: full.at[me_r], lambda m, d: full.at[m])
+
+    def backward(p):
+        high, stride = tall[p], tall[p] + SUB
+        half_n = 8
+        for g in range(per_n[p] // half_n):
+            ns = range(g * half_n, (g + 1) * half_n)
+
+            def step(i, carry, g=g, ns=ns):
+                grads, rates = carry
+                t = length[p] - 1 - i
+                at = tile(t)
+                pace = [pace_t[p, h, at, :] for h in range(eh)]
+                drive = [drive_t[p, h, at, :] for h in range(eh)]
+                gs = [bufs[h, at, :] for h in range(eh)]
+                dd = [bufs[2 + h, at, :] if g else None for h in range(eh)]
+                dp = [bufs[4 + h, at, :] if g else None for h in range(eh)]
+                new, new_rates = [], []
+                for i, n in enumerate(ns):
+                    row = tile(n * (high // SUB) + t)
+                    earlier = tile(n * (stride // SUB) + t)
+                    current = tile(n * (stride // SUB) + t + 1)
+                    source, probe = wide[p, 0, row, :], wide[p, 1, row, :]
+                    flow = read = None
+                    for h in range(eh):
+                        j = i * eh + h
+                        rate = rate_s[p, h, n * SUB : (n + 1) * SUB, :]
+                        grad = grads[j] + probe * gs[h]
+                        term = grad * drive[h]
+                        flow = term if flow is None else flow + term
+                        term = gs[h] * hist[p, h, current, :]
+                        read = term if read is None else read + term
+                        term = grad * source
+                        dd[h] = term if dd[h] is None else dd[h] + term
+                        carried = jnp.exp2(pace[h] * rate) * grad
+                        q = carried * hist[p, h, earlier, :]
+                        term = q * rate
+                        dp[h] = term if dp[h] is None else dp[h] + term
+                        new_rates.append(rates[j] + q * pace[h])
+                        new.append(carried)
+                    wide[p, 0, row, :] = flow
+                    wide[p, 1, row, :] = read
+                for h in range(eh):
+                    bufs[2 + h, at, :] = dd[h]
+                    bufs[4 + h, at, :] = dp[h]
+                return tuple(new), tuple(new_rates)
+
+            chains = (zero,) * (half_n * eh)
+            unused, rates = lax.fori_loop(0, length[p], step, (chains, chains), unroll=2)
+            for i, n in enumerate(ns):
+                for h in range(eh):
+                    place = slice(n * SUB, (n + 1) * SUB)
+                    dr_s[h, place, :] = rates[i * eh + h] * rate_s[p, h, place, :] * (1.0 / LOG2E)
+
+    def finish_pair(p, gate16):
+        lot = p
+        high = tall[p]
+        chunk = count
+        for s in range(high // chunk):
+            flow = jnp.zeros((chunk, LANES), f32)
+            for q in range(per_n[p]):
+                w, n1 = 2 * q // per_n[p], 2 * q % per_n[p]
+                at = n1 * high + s * chunk
+                left = jnp.concatenate(
+                    [wide[p, w, at : at + chunk, :].astype(bf16),
+                     wide[p, w, at + high : at + high + chunk, :].astype(bf16)], axis=1
+                )
+                flow = flow + back(left, spreads[p][:, 2 * q * LANES : 2 * (q + 1) * LANES])
+            probe_t[s * chunk : (s + 1) * chunk, :] = jnp.where(keep_lanes(p, chunk), flow, 0.0)
+
+        def put_flow(k, at, x):
+            bufs[k, at, :] = x
+
+        from_scan(p, lambda at: probe_t[at, :], put_flow)
+        value16 = value_s[p]
+        value = value16.astype(f32)
+        d_total = dval[p]
+        direct = jnp.sum(d_total * value, axis=0, keepdims=True)
+        small = [direct[:, part(h)] for h in range(eh)]
+        skip = skip_ref[2 * p : 2 * p + 1, :] + skip_ref[2 * p + 1 : 2 * p + 2, :]
+        dv = skip * d_total
+        ddt, dpt = [[None] * eh for k in range(2)], [[None] * eh for k in range(2)]
+        for h in range(eh):
+            for which, out in ((2, ddt), (4, dpt)):
+
+                def put_tok(k, at, x, which=which, h=h):
+                    bufs_tok[k, which // 2 - 1, h, at, :] = x
+
+                from_scan(p, lambda at, which=which, h=h: bufs[which + h, at, :], put_tok)
+        for k in range(2):
+            d = 2 * p + k
+            drive = jnp.concatenate([bufs_tok[k, 0, h] for h in range(eh)], axis=1)
+            pull = jnp.concatenate([bufs_tok[k, 1, h] for h in range(eh)], axis=1)
+            pace = jnp.concatenate([tok[p, k, h] for h in range(eh)], axis=1)
+            dv = dv + drive * pace
+            d_before = (drive * value + pull * (1.0 / LOG2E)) * slope[p, k]
+            b_high, b_low = split2(d_before)
+            bias_sum = jnp.sum(d_before, axis=0, keepdims=True)
+            small += [bias_sum[:, part(h)] for h in range(eh)]
+            d_proj = (
+                bufs[k, :count, :] + back(b_high, swp[d, 0]) + back(b_low, swp[d, 0])
+                + back(b_high, swp[d, 1])
+            ).astype(bf16)
+            dv = dv + dot(d_proj, wpk[d])
+            put_wide(lot, cross(proj_s[p, k].astype(bf16), b_high)[2 * states : group])
+            grad = cross(d_proj, value16)
+            put_wide(lot, grad[2 * states : group])
+            put_wide(lot, grad[: 2 * states])
+            for h in range(eh):
+                for m in range(copies_m[p]):
+                    acc = None
+                    for line in range(lines[p]):
+                        s = 2 * line + k if p == 0 else 4 * m + 2 * k + line
+                        term = dr_s[h, pl.ds(s, per_n[p], stride=SUB), :]
+                        acc = term if acc is None else acc + term
+                    put(lot, acc)
+        put(lot, pad_rows(*small))
+        d_val = (dv * silu_slope(mixed_s[p, :, :inner])).astype(bf16)
+        grad = cross(normed_s[p], d_val)
+        if p == 0:
+            in_acc[...] = grad
+            d_mixed = jnp.concatenate([d_val, gate16], axis=1)
+            d_normed = back(d_mixed, in_weight_ref[...])
+        else:
+            put_wide(1, in_acc[...] + grad)
+            d_normed = back(d_val, in_weight_ref[:, :inner])
+        unused, pull = jax.vjp(layer_norm, emb_r[p][...].reshape(count, model), norm_gain_ref[...])
+        d_embedded, norm_grad = pull(d_normed)
+        if p == 0:
+            norm_acc[...] = norm_grad
+        else:
+            put(1, pad_rows(norm_acc[...] + norm_grad))
+        back_s[p][...] = d_embedded.reshape(back_s[p].shape)
+        out = exchange(2, p, back_s[p], back_r[p])
+        pending.extend(out)
+        return out
+
+    arrived(emb1)
+    prologue(1)
+    forward(1)
+    y1 = swap(1, y_s1, y_r0)
+    pending += y1
+    arrived(emb0)
+    prologue(0)
+    forward(0)
+    y0 = swap(0, y_s0, y_r1)
+    pending += y0
+    arrived(y1)
+    arrived(cot0)
+    gate16 = gate(0)
+    backward(0)
+    home0 = finish_pair(0, gate16)
+    early = sum_scatter(0)
+    arrived(y0)
+    arrived(cot1)
+    gate(1)
+    early = sum_across(0, early)
+    backward(1)
+    early = sum_gather(0, early)
+    home1 = finish_pair(1, None)
+    late = sum_scatter(1)
+    arrived(home0)
+    unpack(back_r0, bufs.at[0], 0)
+    home[...] = home[...] + bufs[0, :count, :]
+    late = sum_across(1, late)
+    arrived(home1)
+    unpack(back_r1, bufs.at[1], 1)
+    feature_ref[...] = (home[...] + bufs[1, :count, :]).astype(bf16)
+    arrived(early)
+    late = sum_gather(1, late)
+    arrived(late)
+    sent(pending)
+
+
+def unpack_kernel(
+    states, rank, grad_scale,
+    feature_in, early_ref, late_ref,
+    feature_ref, in_grad_ref, scan_grad_ref, stepw_ref, stepb_ref, dr_ref, skip_grad_ref,
+    norm_grad_ref, gain_grad_ref, out_grad_ref,
+):
+    feature_ref[...] = feature_in[...]
+    inner = out_grad_ref.shape[0]
+    eh = inner // LANES
+    group = rank + 2 * states
+    taken = [0, 0]
+    lots = (early_ref, late_ref)
+
+    def take(lot, height):
+        at = taken[lot]
+        taken[lot] += height
+        return lots[lot][at : at + height, :] * grad_scale
+
+    def take_wide(lot, out, at, height, width):
+        for h in range(width // LANES):
+            out[at : at + height, h * LANES : (h + 1) * LANES] = take(lot, height)
+
+    def part(h):
+        return slice(h * LANES, (h + 1) * LANES)
+
+    for p in range(2):
+        if p == 0:
+            small = take(0, -(-eh // SUB) * SUB)
+            for h in range(eh):
+                gain_grad_ref[:, part(h)] = small[h : h + 1]
+            take_wide(0, out_grad_ref, 0, inner, out_grad_ref.shape[1])
+            for h in range(eh):
+                in_grad_ref[:, inner + h * LANES : inner + (h + 1) * LANES] = take(
+                    0, in_grad_ref.shape[0]
+                )
+        for k in range(2):
+            d = 2 * p + k
+            take_wide(p, stepw_ref.at[d], 0, rank, inner)
+            take_wide(p, scan_grad_ref, d * group, rank, inner)
+            take_wide(p, scan_grad_ref, d * group + rank, 2 * states, inner)
+            take_wide(p, dr_ref.at[d], 0, states, inner)
+        small = take(p, -(-3 * eh // SUB) * SUB)
+        for h in range(eh):
+            for k in range(2):
+                d = 2 * p + k
+                skip_grad_ref[d : d + 1, part(h)] = small[h : h + 1]
+                stepb_ref[d : d + 1, part(h)] = small[(k + 1) * eh + h : (k + 1) * eh + h + 1]
+        if p == 1:
+            take_wide(1, in_grad_ref, 0, in_grad_ref.shape[0], inner)
+            norm_grad_ref[...] = take(1, SUB)[0:1]
+
+
+def fast(
+    classes, features, cotangent, table, norm_gain, in_weight, scan_weight, step_weight,
+    step_bias, decay_log, skip_gain, output_gain, output_weight,
+):
+    tile_rows, tile_cols, model = features.shape
+    inner = output_weight.shape[0]
+    count = tile_rows * tile_cols
+    rows, cols = lax.axis_size("row"), lax.axis_size("col")
+    rank, states = step_weight.shape[1], decay_log.shape[1]
+    group = rank + 2 * states
+    eh = inner // LANES
+    grad_scale = float(count * rows * cols) ** (-0.5)
+    embedded = embed(features, classes, table).reshape(count, model)
+    f32, bf16 = jnp.float32, jnp.bfloat16
+    tall = max(SUB * count // (tile_rows // cols), SUB * count // (tile_cols // rows))
+    blocks = count // SUB
+    early, late = lots_of(rows, inner, model, states, rank, group, eh)
+    per_row = ((cols, count // cols, model), (rows, count // rows, model))
+    scratch = [((count, model), f32)]
+    for name in range(6):
+        scratch += [(per_row[0], f32), (per_row[1], f32)]
+    scratch += [((blocks, SUB, inner), f32)] * 4
+    scratch += [
+        ((LANES, 2 * states * LANES), bf16),
+        ((LANES, 2 * states * LANES // 2), bf16),
+        ((4, LANES, inner), bf16),
+        ((4, 2, LANES, inner), bf16),
+        ((4, 2, inner, inner), bf16),
+        ((2, eh, states * SUB, LANES), f32),
+        ((2, count, model), bf16),
+        ((2, count, 2 * inner), f32),
+        ((2, count, inner), bf16),
+        ((2, 2, count, LANES), f32),
+        ((2, 2, eh, count, LANES), f32),
+        ((2, 2, count, inner), f32),
+        ((2, 2, 2 * count * states, LANES), f32),
+        ((2, eh, 2 * count * states + states * SUB, LANES), f32),
+        ((2, eh, tall, LANES), f32),
+        ((2, eh, tall, LANES), f32),
+        ((6, tall, LANES), f32),
+        ((2, 2, eh, count, LANES), f32),
+        ((tall, LANES), f32),
+        ((tall, LANES), bf16),
+        ((2, count, inner), f32),
+        ((eh, states * SUB, LANES), f32),
+        ((model, inner), f32),
+        ((1, model), f32),
+    ]
+    for lot in (early, late):
+        chunk = (lot // rows, LANES)
+        scratch += [((rows,) + chunk, f32), ((rows - 1,) + chunk, f32), ((cols,) + chunk, f32)]
+    feature, early_sum, late_sum = pl.pallas_call(
+        functools.partial(fast_kernel, tile_rows, tile_cols, states, rank),
+        out_shape=[
+            jax.ShapeDtypeStruct((count, model), bf16),
+            jax.ShapeDtypeStruct((rows, early // rows, LANES), f32),
+            jax.ShapeDtypeStruct((rows, late // rows, LANES), f32),
+        ],
+        in_specs=[VMEM] * 11,
+        out_specs=[VMEM] * 3,
+        scratch_shapes=[pltpu.VMEM(*s) for s in scratch]
+        + [
+            pltpu.SemaphoreType.DMA((3, 2, 2, max(rows, cols))),
+            pltpu.SemaphoreType.DMA((2, 2, rows * cols)),
+            pltpu.SemaphoreType.DMA((2, 3, 2, max(rows, cols))),
+        ],
+        compiler_params=pltpu.CompilerParams(
+            vmem_limit_bytes=BIG, collective_id=1, has_side_effects=True
+        ),
+    )(
+        embedded, cotangent.reshape(count, model), norm_gain[None], in_weight, scan_weight.T,
+        step_weight, step_bias, decay_log, skip_gain, output_gain[None], output_weight,
+    )
+    shapes = [
+        ((count, model), bf16),
+        (in_weight.shape, f32),
+        (scan_weight.shape[::-1], f32),
+        (step_weight.shape, f32),
+        (step_bias.shape, f32),
+        (decay_log.shape, f32),
+        (skip_gain.shape, f32),
+        ((1, model), f32),
+        ((1, inner), f32),
+        (output_weight.shape, f32),
+    ]
+    feature_grad, *grads = pl.pallas_call(
+        functools.partial(unpack_kernel, states, rank, grad_scale),
+        out_shape=[jax.ShapeDtypeStruct(*s) for s in shapes],
+        in_specs=[VMEM] * 3,
+        out_specs=[VMEM] * 10,
+    )(feature, early_sum.reshape(early, LANES), late_sum.reshape(late, LANES))
+    feature_grad = feature_grad.reshape(tile_rows, tile_cols, model)
+    grads[1] = grads[1].T
+    grads[6], grads[7] = grads[6][0], grads[7][0]
+    return (feature_grad, *grads)
+
+
+def local(*args):
+    tile_rows, tile_cols, model = args[1].shape
+    rows, cols = lax.axis_size("row"), lax.axis_size("col")
+    rank, states, inner = args[7].shape[1], args[9].shape[1], args[12].shape[0]
+    fits = (
+        tile_rows == 4 * cols and tile_cols == 2 * rows and model == LANES and inner == 2 * LANES
+        and states == 2 * SUB and rank == SUB
+    )
+    return (fast if fits else general)(*args)
+
+
 def solution(mesh):
     in_specs = (P("row", "col"), P("row", "col", None), P("row", "col", None)) + (P(),) * 10
     out_specs = (P("row", "col", None),) + (P(),) * 9

time: 99.6 us -> 82.9 us (0.83)
  Pallas kernels: 87.8 us -> 79.6 us
  local copies, waits for them, and re-layouts: 8.37 us -> 0.7 us
  other arithmetic: 1.52 us -> 0 us
    pallas_call x1 -> x2, Pallas kernels: 87.8 us -> 79.6 us  [the longest x1 77.5 us: fast(): pl.pallas_call(functools.partial(fast_kernel, tile_rows, tile_cols, state...]
    unnamed x37 -> x2, local copies, waits for them, and re-layouts: 8.37 us -> 0.7 us
    mul x1 -> x0, other arithmetic: 1.52 us -> none  [local(): rate2 = -jnp.exp(decay_log) * LOG2E]
where the time goes in v1:
time: 82.9 us; the launch traced here: 82.7 us
  Pallas kernels  79.6 us (96%)
  matrix products  1.77 us (2%)
    pallas_call x1, Pallas kernels, fast(): pl.pallas_call(functools.partial(fast_kernel, tile_rows, tile_cols, state...  77.5 us
    pallas_call x1, Pallas kernels, fast(): pl.pallas_call(functools.partial(unpack_kernel, states, rank, grad_scale)...  2.02 us
    dot_general x1, matrix products, embed(): lookup = jnp.einsum('hwk,kd->hwd', onehot, table, precision=HIGHEST)  1.77 us

profile of v1, /device:TPU:0, one launch (start us, length us, event | category | flops | bytes accessed | tf_op | source)
XLA Modules:
  0.0 82.7 jit_solution(13410419670050531361)
XLA Ops:
  0.6 0.0 copy-start
  0.7 0.7 copy-done
  1.3 1.8 %convolution_add_fusion = f32[16,16,128]{2,1,0:T(8,128)} fusion(bf16[16,16,128]{2,1,0:T(8,128)(2,1)} %param.14, s32[16,16]{1,0:T(8,128)} %param.13, f32[16,128]{1,0:T(8,128)S(1)} %copy-done), kind=kOutput, calls=%fused_computation | convolution fusion | flops 6361088 | bytes 205824 | tf_op jit(solution)/shard_map/hwk,kd->hwd/dot_general | solution.py:36
  3.1 77.5 %shard_map.204 = (bf16[256,128]{1,0:T(8,128)(2,1)}, f32[8,104,128]{2,1,0:T(8,128)}, f32[8,72,128]{2,1,0:T(8,128)}) custom-call(f32[256,128]{1,0:T(8,128)} %bitcast.14, bf16[256,128]{1,0:T(8,128)(2,1)} %bitcast.18, f32[1,128]{1,0:T(1,128)} %bitcast.20, bf16[128,512]{1,0:T(8,128)(2,1)} %in_weight_ref.1, bf16[160,256]{1,0:T(8,128)(2,1)} %bitcast.17, ...), custom_call_target="tpu_custom_call" | custom-call | tf_op jit(solution)/shard_map/pallas_call | solution.py:1331
  80.7 2.0 %shard_map.205 = (bf16[256,128]{1,0:T(8,128)(2,1)}, f32[128,512]{1,0:T(8,128)}, f32[160,256]{1,0:T(8,128)}, f32[4,8,256]{2,1,0:T(8,128)}, f32[4,256]{1,0:T(4,128...) custom-call(bf16[256,128]{1,0:T(8,128)(2,1)} %get-tuple-element.23.f, ...), custom_call_target="tpu_custom_call" | custom-call | tf_op jit(solution)/shard_map/pallas_call | solution.py:1365
Async XLA Ops:
  0.6 0.7 copy-start

commit v2 on v1

--- a/solution.py
+++ b/solution.py
@@ -610,28 +610,27 @@
 
 
 def lots_of(rows, inner, model_width, states, rank, group, eh):
-    small = -(-5 * eh // SUB) * SUB
-    pair = 2 * (rank + states) * eh + small + 2 * group * eh
-    early = inner * model_width // LANES + model_width * eh + SUB + pair
-    late = model_width * eh + SUB + pair
+    pair = (rank + states + group) * 2 * eh + -(-3 * eh // SUB) * SUB
+    gated = SUB + inner * model_width // LANES + model_width * eh
     per = SUB * rows
-    return tuple(-(-n // per) * per for n in (early, late))
+    return tuple(-(-n // per) * per for n in (gated, pair, pair, model_width * eh + SUB))
 
 
 def fast_kernel(
     tile_rows, tile_cols, states, rank,
-    embedded_ref, upstream_ref, norm_gain_ref, in_weight_ref, sw_ref, step_weight_ref,
-    step_bias_ref, decay_ref, skip_ref, output_gain_ref, output_weight_ref,
-    feature_ref, early_ref, late_ref,
+    features_ref, classes_ref, table_ref, upstream_ref, norm_gain_ref, in_weight_ref, sw_ref,
+    step_weight_ref, step_bias_ref, decay_ref, skip_ref, output_gain_ref, output_weight_ref,
+    feature_ref, full0, full1, full2, full3,
     home, emb_s0, emb_s1, emb_r0, emb_r1, cot_s0, cot_s1, cot_r0, cot_r1,
     back_s0, back_s1, back_r0, back_r1, y_s0, y_s1, y_r0, y_r1,
     spread0, spread1, wpk, swp, cmat, rate_s, normed_s, mixed_s, value_s, proj_s, tok, slope,
-    wide, hist, pace_t, drive_t, bufs, bufs_tok, probe_t, lhs, dval, dr_s, in_acc, norm_acc,
-    mine0, from0, side0, mine1, from1, side1, sems, ysems, sumsems,
+    wide, flows, hist, pace_t, drive_t, g_t, dd_a, dd_b, dp_a, dp_b, bufs, bufs_tok, probe_t, lhs, dval, dr_s, in_acc, norm_acc,
+    mine0, from0, side0, mine1, from1, side1, mine2, from2, side2, mine3, from3, side3,
+    sems, ysems, sumsems,
 ):
     f32, bf16 = jnp.float32, jnp.bfloat16
     count, inner = tile_rows * tile_cols, output_weight_ref.shape[0]
-    model = embedded_ref.shape[1]
+    model = features_ref.shape[1]
     rows, cols = lax.axis_size("row"), lax.axis_size("col")
     me_r, me_c = lax.axis_index("row"), lax.axis_index("col")
     eh = inner // LANES
@@ -658,6 +657,9 @@
     def tile(b):
         return pl.ds(pl.multiple_of(b * SUB, SUB), SUB)
 
+    def tile2(b):
+        return pl.ds(pl.multiple_of(b * 2 * SUB, 2 * SUB), 2 * SUB)
+
     greet_all()
 
     def pack(src, dst, p):
@@ -690,27 +692,30 @@
                         r, pl.ds(j, tile_rows, stride=2), :
                     ]
 
+    def batch(src, dst, amount, send, recv):
+        return pltpu.make_async_remote_copy(
+            src_ref=src.at[pl.ds(0, amount)], dst_ref=dst.at[pl.ds(0, amount)], send_sem=send,
+            recv_sem=recv, device_id={"row": me_r, "col": me_c}, device_id_type=MESH,
+        )
+
     def exchange(turn, p, src, dst):
         size, axis = sizes[p], axes[p]
         me = lax.axis_index(axis)
-        out = []
         for d in range(1, size):
             target = lax.rem(me + d, size)
             copy = pltpu.make_async_remote_copy(
                 src_ref=src.at[target],
                 dst_ref=dst.at[me],
-                send_sem=sems.at[turn, p, 0, d],
-                recv_sem=sems.at[turn, p, 1, d],
+                send_sem=sems.at[turn, p, 0],
+                recv_sem=sems.at[turn, p, 1],
                 device_id={axis: target},
                 device_id_type=MESH,
             )
             copy.start()
-            out.append(copy)
         dst[me] = src[me]
-        return out
+        return [batch(src, dst, size - 1, sems.at[turn, p, 0], sems.at[turn, p, 1])]
 
     def swap(p, src, dst):
-        out = []
         for dr in range(rows):
             for dc in range(cols):
                 r, c = lax.rem(me_r + dr, rows), lax.rem(me_c + dc, cols)
@@ -724,14 +729,13 @@
                 copy = pltpu.make_async_remote_copy(
                     src_ref=src.at[there],
                     dst_ref=dst.at[here],
-                    send_sem=ysems.at[p, 0, dr * cols + dc],
-                    recv_sem=ysems.at[p, 1, dr * cols + dc],
+                    send_sem=ysems.at[p, 0],
+                    recv_sem=ysems.at[p, 1],
                     device_id={"row": r, "col": c},
                     device_id_type=MESH,
                 )
                 copy.start()
-                out.append(copy)
-        return out
+        return [batch(src, dst, rows * cols - 1, ysems.at[p, 0], ysems.at[p, 1])]
 
     def arrived(copies):
         for copy in copies:
@@ -747,10 +751,38 @@
     y_s, y_r = (y_s0, y_s1), (y_r0, y_r1)
     spreads = (spread0, spread1)
     pending = []
-
-    pack(embedded_ref, emb_s1, 1)
+    half_n = SUB
+    dd_t, dp_t = (dd_a, dd_b), (dp_a, dp_b)
+    y_t = dd_t
+
+    def added(refs, p, h, at):
+        total = refs[0][h, at, :]
+        for g in range(1, per_n[p] // half_n):
+            total = total + refs[g][h, at, :]
+        return total
+
+    token = lax.broadcasted_iota(jnp.int32, (count, tile_rows), 0)
+    lane = lax.broadcasted_iota(jnp.int32, (count, tile_rows), 1)
+    of_row = jnp.where(token // tile_cols == lane, 1.0, 0.0).astype(bf16)
+    labels = dot(of_row, classes_ref[...].astype(f32).astype(bf16))
+    token = lax.broadcasted_iota(jnp.int32, (count, tile_cols), 0)
+    lane = lax.broadcasted_iota(jnp.int32, (count, tile_cols), 1)
+    labels = jnp.where(lax.rem(token, tile_cols) == lane, labels, 0.0).astype(bf16)
+    labels = dot(labels, jnp.ones((tile_cols, LANES), bf16))
+    lane = lax.broadcasted_iota(jnp.int32, (count, LANES), 1).astype(f32)
+    onehot = jnp.where(labels == lane, 1.0, 0.0).astype(bf16)
+    entries = table_ref[...]
+    lookup = None
+    for i in range(3):
+        rounded = entries.astype(bf16).astype(f32)
+        rest = jnp.zeros((LANES - entries.shape[0], model), f32)
+        term = dot(onehot, jnp.concatenate([rounded, rest], axis=0).astype(bf16))
+        lookup = term if lookup is None else lookup + term
+        entries = entries - rounded
+    home[...] = features_ref[...].astype(f32) + lookup
+    pack(home, emb_s1, 1)
     emb1 = exchange(0, 1, emb_s1, emb_r1)
-    pack(embedded_ref, emb_s0, 0)
+    pack(home, emb_s0, 0)
     emb0 = exchange(0, 0, emb_s0, emb_r0)
     home[...] = upstream_ref[...].astype(f32)
     pack(home, cot_s0, 0)
@@ -809,8 +841,13 @@
                 else:
                     rate_s[p, h, at, :] = jnp.where(mask, row, rate_s[p, h, at, :])
 
-    def to_scan(p, first, second, store):
+    def to_scan(p, *moves):
         def one(b, carry):
+            for move in moves:
+                one_of(b, *move)
+            return carry
+
+        def one_of(b, first, second, store):
             mirror = blocks - 1 - b
             x0, x1 = first(tile(b)), second(tile(mirror))
             if p == 0:
@@ -829,12 +866,16 @@
                 store(tile(4 * b + 1), jnp.where(low_half, v2, u2))
                 store(tile(4 * b + 2), jnp.where(pos_edge, v, u))
                 store(tile(4 * b + 3), jnp.where(low_half, u2, v2))
+
+        lax.fori_loop(0, blocks, one, 0, unroll=max(2, 4 // len(moves)))
+
+    def from_scan(p, *moves):
+        def one(b, carry):
+            for move in moves:
+                one_of(b, *move)
             return carry
 
-        lax.fori_loop(0, blocks, one, 0, unroll=4)
-
-    def from_scan(p, load, store):
-        def one(b, carry):
+        def one_of(b, load, store):
             mirror = blocks - 1 - b
             if p == 0:
                 s0, s1 = load(tile(2 * b)), load(tile(2 * b + 1))
@@ -854,9 +895,14 @@
                     1, tile(mirror),
                     jnp.where(low_half, jnp.where(pos == 0, a[3], a[2]), jnp.where(pos == 2, a[1], a[0])),
                 )
-            return carry
-
-        lax.fori_loop(0, blocks, one, 0, unroll=4)
+
+        lax.fori_loop(0, blocks, one, 0, unroll=max(2, 4 // len(moves)))
+
+    def put_at(ref, at, x):
+        ref[at, :] = x
+
+    def put_probe(at, x):
+        probe_t[at, :] = x
 
     def prologue(p):
         embedded = emb_r[p][...].reshape(count, model)
@@ -874,23 +920,19 @@
             pace = softplus(before)
             for h in range(eh):
                 tok[p, k, h] = pace[:, part(h)]
+        moves = [(lambda at: proj_s[p, 0, at, :], lambda at: proj_s[p, 1, at, :], put_probe)]
         for h in range(eh):
-            for k in range(2):
-                bufs[k, :count, :] = tok[p, k, h] * value32[:, part(h)]
-
-            def put_pace(at, x, h=h):
-                pace_t[p, h, at, :] = x
-
-            def put_drive(at, x, h=h):
-                drive_t[p, h, at, :] = x
-
-            to_scan(p, lambda at, h=h: tok[p, 0, h, at, :], lambda at, h=h: tok[p, 1, h, at, :], put_pace)
-            to_scan(p, lambda at: bufs[0, at, :], lambda at: bufs[1, at, :], put_drive)
-
-        def put_probe(at, x):
-            probe_t[at, :] = x
-
-        to_scan(p, lambda at: proj_s[p, 0, at, :], lambda at: proj_s[p, 1, at, :], put_probe)
+            bufs_tok[0, 0, h] = value32[:, part(h)]
+            moves.append(
+                (lambda at, h=h: tok[p, 0, h, at, :], lambda at, h=h: tok[p, 1, h, at, :],
+                 functools.partial(put_at, pace_t.at[p, h]))
+            )
+            moves.append(
+                (lambda at, h=h: tok[p, 0, h, at, :] * bufs_tok[0, 0, h, at, :],
+                 lambda at, h=h: tok[p, 1, h, at, :] * bufs_tok[0, 0, h, at, :],
+                 functools.partial(put_at, drive_t.at[p, h]))
+            )
+        to_scan(p, *moves)
         size_of = tall[p]
         x = jnp.where(keep_lanes(p, size_of), probe_t[:size_of, :], 0.0)
         high = x.astype(bf16).astype(f32)
@@ -918,7 +960,6 @@
 
     def forward(p):
         high, stride = tall[p], tall[p] + SUB
-        half_n = 8
         for h in range(eh):
             for n in range(per_n[p]):
                 hist[p, h, n * stride : n * stride + SUB, :] = zero
@@ -930,7 +971,7 @@
                 at = tile(t)
                 pace = [pace_t[p, h, at, :] for h in range(eh)]
                 drive = [drive_t[p, h, at, :] for h in range(eh)]
-                y = [bufs[h, at, :] if g else None for h in range(eh)]
+                y = [None] * eh
                 new = []
                 for i, n in enumerate(ns):
                     row = tile(n * (high // SUB) + t)
@@ -944,17 +985,20 @@
                         term = probe * state
                         y[h] = term if y[h] is None else y[h] + term
                 for h in range(eh):
-                    bufs[h, at, :] = y[h]
+                    y_t[g][h, at, :] = y[h]
                 return tuple(new)
 
             lax.fori_loop(0, length[p], step, (zero,) * (half_n * eh), unroll=2)
+        moves = []
         for h in range(eh):
 
             def put_y(k, at, x, h=h):
-                bufs[2 + k, at, :] = x
-
-            from_scan(p, lambda at, h=h: bufs[h, at, :], put_y)
-            y_s[p][:, :, part(h)] = (bufs[2, :count, :] + bufs[3, :count, :]).reshape(blocks, SUB, LANES)
+                bufs_tok[k, 0, h, at, :] = x
+
+            moves.append((lambda at, h=h: added(y_t, p, h, at), put_y))
+        from_scan(p, *moves)
+        for h in range(eh):
+            y_s[p][:, :, part(h)] = (bufs_tok[0, 0, h] + bufs_tok[1, 0, h]).reshape(blocks, SUB, LANES)
 
     def gate(p):
         value = value_s[p].astype(f32)
@@ -976,18 +1020,18 @@
         else:
             gate16 = None
 
+        moves = []
         for h in range(eh):
-
-            def put_g(at, x, h=h):
-                bufs[h, at, :] = x
-
-            to_scan(
-                p, lambda at, h=h: dval[p, at, part(h)], lambda at, h=h: dval[p, at, part(h)], put_g
-            )
+            load = lambda at, h=h: dval[p, at, part(h)]
+            moves.append((load, load, functools.partial(put_at, g_t.at[h])))
+        to_scan(p, *moves)
         return gate16
 
-    sums = ((mine0, from0, side0, early_ref), (mine1, from1, side1, late_ref))
-    fill = [0, 0]
+    sums = (
+        (mine0, from0, side0, full0), (mine1, from1, side1, full1),
+        (mine2, from2, side2, full2), (mine3, from3, side3, full3),
+    )
+    fill = [0] * 4
 
     def put(lot, x):
         mine = sums[lot][0]
@@ -1011,29 +1055,28 @@
         while fill[lot] < rows * mine.shape[1] // SUB:
             put(lot, zero)
 
-    def spread(lot, phase, axis, source, result):
+    def spread(lot, phase, axis, source, result, whole):
         size = lax.axis_size(axis)
         me = lax.axis_index(axis)
-        out = []
         for d in range(1, size):
             target = lax.rem(me + d, size)
             copy = pltpu.make_async_remote_copy(
                 src_ref=source(target),
                 dst_ref=result(me, d),
-                send_sem=sumsems.at[lot, phase, 0, d],
-                recv_sem=sumsems.at[lot, phase, 1, d],
+                send_sem=sumsems.at[lot, phase, 0],
+                recv_sem=sumsems.at[lot, phase, 1],
                 device_id={axis: target},
                 device_id_type=MESH,
             )
             copy.start()
-            out.append(copy)
+        out = [batch(whole, whole, size - 1, sumsems.at[lot, phase, 0], sumsems.at[lot, phase, 1])]
         pending.extend(out)
         return out
 
     def sum_scatter(lot):
         mine, other, side, full = sums[lot]
         pad_lot(lot)
-        return spread(lot, 0, "row", lambda t: mine.at[t], lambda me, d: other.at[d - 1])
+        return spread(lot, 0, "row", lambda t: mine.at[t], lambda me, d: other.at[d - 1], other)
 
     def sum_across(lot, copies):
         mine, other, side, full = sums[lot]
@@ -1042,7 +1085,7 @@
         for d in range(rows - 1):
             acc = acc + other[d]
         side[me_c] = acc
-        return spread(lot, 1, "col", lambda t: side.at[me_c], lambda m, d: side.at[m])
+        return spread(lot, 1, "col", lambda t: side.at[me_c], lambda m, d: side.at[m], side)
 
     def sum_gather(lot, copies):
         mine, other, side, full = sums[lot]
@@ -1051,23 +1094,20 @@
         for d in range(1, cols):
             acc = acc + side[d]
         full[me_r] = acc
-        return spread(lot, 2, "row", lambda t: full.at[me_r], lambda m, d: full.at[m])
+        return spread(lot, 2, "row", lambda t: full.at[me_r], lambda m, d: full.at[m], full)
 
     def backward(p):
         high, stride = tall[p], tall[p] + SUB
-        half_n = 8
         for g in range(per_n[p] // half_n):
             ns = range(g * half_n, (g + 1) * half_n)
 
             def step(i, carry, g=g, ns=ns):
-                grads, rates = carry
-                t = length[p] - 1 - i
+                grads, rates, t = carry
                 at = tile(t)
                 pace = [pace_t[p, h, at, :] for h in range(eh)]
                 drive = [drive_t[p, h, at, :] for h in range(eh)]
-                gs = [bufs[h, at, :] for h in range(eh)]
-                dd = [bufs[2 + h, at, :] if g else None for h in range(eh)]
-                dp = [bufs[4 + h, at, :] if g else None for h in range(eh)]
+                gs = [g_t[h, at, :] for h in range(eh)]
+                dd, dp = [None] * eh, [None] * eh
                 new, new_rates = [], []
                 for i, n in enumerate(ns):
                     row = tile(n * (high // SUB) + t)
@@ -1091,40 +1131,57 @@
                         dp[h] = term if dp[h] is None else dp[h] + term
                         new_rates.append(rates[j] + q * pace[h])
                         new.append(carried)
-                    wide[p, 0, row, :] = flow
-                    wide[p, 1, row, :] = read
+                    if n % 2 == 0:
+                        kept = (flow, read)
+                        continue
+                    place = tile2((n // 2) * (high // SUB) + t)
+                    for w, x in enumerate((flow, read)):
+                        both = jnp.concatenate([kept[w], x], axis=0)
+                        flows[w, place, :] = both.astype(bf16)
                 for h in range(eh):
-                    bufs[2 + h, at, :] = dd[h]
-                    bufs[4 + h, at, :] = dp[h]
-                return tuple(new), tuple(new_rates)
+                    dd_t[g][h, at, :] = dd[h]
+                    dp_t[g][h, at, :] = dp[h]
+                return tuple(new), tuple(new_rates), t - 1
 
             chains = (zero,) * (half_n * eh)
-            unused, rates = lax.fori_loop(0, length[p], step, (chains, chains), unroll=2)
+            unused, rates, end = lax.fori_loop(
+                0, length[p], step, (chains, chains, jnp.int32(length[p] - 1)), unroll=2
+            )
             for i, n in enumerate(ns):
                 for h in range(eh):
                     place = slice(n * SUB, (n + 1) * SUB)
                     dr_s[h, place, :] = rates[i * eh + h] * rate_s[p, h, place, :] * (1.0 / LOG2E)
 
     def finish_pair(p, gate16):
-        lot = p
+        lot = p + 1
         high = tall[p]
         chunk = count
+        wide_high = 2 * chunk
+        lane = lax.broadcasted_iota(jnp.int32, (wide_high, LANES), 1)
+        row = lax.broadcasted_iota(jnp.int32, (wide_high, LANES), 0)
+        mine = lax.rem(lane, 2) == lax.rem(row // SUB, 2)
+        keep = keep_lanes(p, wide_high) & mine
+
+        def ones_of(w, a):
+            at = (w * per_n[p] + 2 * a) * LANES
+            return spreads[p][:, at : at + LANES] + spreads[p][:, at + LANES : at + 2 * LANES]
+
         for s in range(high // chunk):
-            flow = jnp.zeros((chunk, LANES), f32)
-            for q in range(per_n[p]):
-                w, n1 = 2 * q // per_n[p], 2 * q % per_n[p]
-                at = n1 * high + s * chunk
-                left = jnp.concatenate(
-                    [wide[p, w, at : at + chunk, :].astype(bf16),
-                     wide[p, w, at + high : at + high + chunk, :].astype(bf16)], axis=1
-                )
-                flow = flow + back(left, spreads[p][:, 2 * q * LANES : 2 * (q + 1) * LANES])
-            probe_t[s * chunk : (s + 1) * chunk, :] = jnp.where(keep_lanes(p, chunk), flow, 0.0)
+            flow = None
+            for w in range(2):
+                for a in range(0, per_n[p] // 2, 2):
+                    at = [(a + i) * 2 * high + s * wide_high for i in range(2)]
+                    left = jnp.concatenate([flows[w, i : i + wide_high, :] for i in at], axis=1)
+                    right = jnp.concatenate([ones_of(w, a), ones_of(w, a + 1)], axis=1)
+                    term = back(left, right)
+                    flow = term if flow is None else flow + term
+            flow = jnp.where(keep, flow, 0.0).reshape(chunk // SUB, 2, SUB, LANES)
+            probe_t[s * chunk : (s + 1) * chunk, :] = (flow[:, 0] + flow[:, 1]).reshape(chunk, LANES)
 
         def put_flow(k, at, x):
             bufs[k, at, :] = x
 
-        from_scan(p, lambda at: probe_t[at, :], put_flow)
+        moves = [(lambda at: probe_t[at, :], put_flow)]
         value16 = value_s[p]
         value = value16.astype(f32)
         d_total = dval[p]
@@ -1132,14 +1189,14 @@
         small = [direct[:, part(h)] for h in range(eh)]
         skip = skip_ref[2 * p : 2 * p + 1, :] + skip_ref[2 * p + 1 : 2 * p + 2, :]
         dv = skip * d_total
-        ddt, dpt = [[None] * eh for k in range(2)], [[None] * eh for k in range(2)]
         for h in range(eh):
-            for which, out in ((2, ddt), (4, dpt)):
+            for which, source in enumerate((dd_t, dp_t)):
 
                 def put_tok(k, at, x, which=which, h=h):
-                    bufs_tok[k, which // 2 - 1, h, at, :] = x
-
-                from_scan(p, lambda at, which=which, h=h: bufs[which + h, at, :], put_tok)
+                    bufs_tok[k, which, h, at, :] = x
+
+                moves.append((lambda at, source=source, h=h: added(source, p, h, at), put_tok))
+        from_scan(p, *moves)
         for k in range(2):
             d = 2 * p + k
             drive = jnp.concatenate([bufs_tok[k, 0, h] for h in range(eh)], axis=1)
@@ -1168,6 +1225,9 @@
                         acc = term if acc is None else acc + term
                     put(lot, acc)
         put(lot, pad_rows(*small))
+        steps = [sum_scatter(lot)]
+        if p == 1:
+            between()
         d_val = (dv * silu_slope(mixed_s[p, :, :inner])).astype(bf16)
         grad = cross(normed_s[p], d_val)
         if p == 0:
@@ -1175,18 +1235,19 @@
             d_mixed = jnp.concatenate([d_val, gate16], axis=1)
             d_normed = back(d_mixed, in_weight_ref[...])
         else:
-            put_wide(1, in_acc[...] + grad)
+            put_wide(3, in_acc[...] + grad)
             d_normed = back(d_val, in_weight_ref[:, :inner])
         unused, pull = jax.vjp(layer_norm, emb_r[p][...].reshape(count, model), norm_gain_ref[...])
         d_embedded, norm_grad = pull(d_normed)
         if p == 0:
             norm_acc[...] = norm_grad
         else:
-            put(1, pad_rows(norm_acc[...] + norm_grad))
+            put(3, pad_rows(norm_acc[...] + norm_grad))
+            steps.append(sum_scatter(3))
         back_s[p][...] = d_embedded.reshape(back_s[p].shape)
         out = exchange(2, p, back_s[p], back_r[p])
         pending.extend(out)
-        return out
+        return [out] + steps
 
     arrived(emb1)
     prologue(1)
@@ -1201,33 +1262,42 @@
     arrived(y1)
     arrived(cot0)
     gate16 = gate(0)
+    first = sum_scatter(0)
     backward(0)
-    home0 = finish_pair(0, gate16)
-    early = sum_scatter(0)
+    first = sum_across(0, first)
+    home0, second = finish_pair(0, gate16)
+    first = sum_gather(0, first)
     arrived(y0)
     arrived(cot1)
     gate(1)
-    early = sum_across(0, early)
     backward(1)
-    early = sum_gather(0, early)
-    home1 = finish_pair(1, None)
-    late = sum_scatter(1)
+    flying = [sum_across(1, second)]
+
+    def between():
+        flying.append(sum_gather(1, flying[0]))
+
+    home1, third, fourth = finish_pair(1, None)
+    sent(pending[:-3])
+    del pending[:-3]
+    third = sum_across(2, third)
+    home[...] = upstream_ref[...].astype(f32)
     arrived(home0)
     unpack(back_r0, bufs.at[0], 0)
     home[...] = home[...] + bufs[0, :count, :]
-    late = sum_across(1, late)
+    fourth = sum_across(3, fourth)
+    third = sum_gather(2, third)
     arrived(home1)
     unpack(back_r1, bufs.at[1], 1)
     feature_ref[...] = (home[...] + bufs[1, :count, :]).astype(bf16)
-    arrived(early)
-    late = sum_gather(1, late)
-    arrived(late)
+    fourth = sum_gather(3, fourth)
+    for copies in (first, flying[1], third, fourth):
+        arrived(copies)
     sent(pending)
 
 
 def unpack_kernel(
     states, rank, grad_scale,
-    feature_in, early_ref, late_ref,
+    feature_in, full0, full1, full2, full3,
     feature_ref, in_grad_ref, scan_grad_ref, stepw_ref, stepb_ref, dr_ref, skip_grad_ref,
     norm_grad_ref, gain_grad_ref, out_grad_ref,
 ):
@@ -1235,8 +1305,8 @@
     inner = out_grad_ref.shape[0]
     eh = inner // LANES
     group = rank + 2 * states
-    taken = [0, 0]
-    lots = (early_ref, late_ref)
+    taken = [0] * 4
+    lots = (full0, full1, full2, full3)
 
     def take(lot, height):
         at = taken[lot]
@@ -1250,31 +1320,29 @@
     def part(h):
         return slice(h * LANES, (h + 1) * LANES)
 
+    small = take(0, SUB)
+    for h in range(eh):
+        gain_grad_ref[:, part(h)] = small[h : h + 1]
+    take_wide(0, out_grad_ref, 0, inner, out_grad_ref.shape[1])
+    model = in_grad_ref.shape[0]
+    for h in range(eh):
+        in_grad_ref[:, inner + h * LANES : inner + (h + 1) * LANES] = take(0, model)
     for p in range(2):
-        if p == 0:
-            small = take(0, -(-eh // SUB) * SUB)
-            for h in range(eh):
-                gain_grad_ref[:, part(h)] = small[h : h + 1]
-            take_wide(0, out_grad_ref, 0, inner, out_grad_ref.shape[1])
-            for h in range(eh):
-                in_grad_ref[:, inner + h * LANES : inner + (h + 1) * LANES] = take(
-                    0, in_grad_ref.shape[0]
-                )
+        lot = p + 1
         for k in range(2):
             d = 2 * p + k
-            take_wide(p, stepw_ref.at[d], 0, rank, inner)
-            take_wide(p, scan_grad_ref, d * group, rank, inner)
-            take_wide(p, scan_grad_ref, d * group + rank, 2 * states, inner)
-            take_wide(p, dr_ref.at[d], 0, states, inner)
-        small = take(p, -(-3 * eh // SUB) * SUB)
+            take_wide(lot, stepw_ref.at[d], 0, rank, inner)
+            take_wide(lot, scan_grad_ref, d * group, rank, inner)
+            take_wide(lot, scan_grad_ref, d * group + rank, 2 * states, inner)
+            take_wide(lot, dr_ref.at[d], 0, states, inner)
+        small = take(lot, -(-3 * eh // SUB) * SUB)
         for h in range(eh):
             for k in range(2):
                 d = 2 * p + k
                 skip_grad_ref[d : d + 1, part(h)] = small[h : h + 1]
                 stepb_ref[d : d + 1, part(h)] = small[(k + 1) * eh + h : (k + 1) * eh + h + 1]
-        if p == 1:
-            take_wide(1, in_grad_ref, 0, in_grad_ref.shape[0], inner)
-            norm_grad_ref[...] = take(1, SUB)[0:1]
+    take_wide(3, in_grad_ref, 0, model, inner)
+    norm_grad_ref[...] = take(3, SUB)[0:1]
 
 
 def fast(
@@ -1289,11 +1357,10 @@
     group = rank + 2 * states
     eh = inner // LANES
     grad_scale = float(count * rows * cols) ** (-0.5)
-    embedded = embed(features, classes, table).reshape(count, model)
     f32, bf16 = jnp.float32, jnp.bfloat16
     tall = max(SUB * count // (tile_rows // cols), SUB * count // (tile_cols // rows))
     blocks = count // SUB
-    early, late = lots_of(rows, inner, model, states, rank, group, eh)
+    lots = lots_of(rows, inner, model, states, rank, group, eh)
     per_row = ((cols, count // cols, model), (rows, count // rows, model))
     scratch = [((count, model), f32)]
     for name in range(6):
@@ -1313,10 +1380,16 @@
         ((2, 2, eh, count, LANES), f32),
         ((2, 2, count, inner), f32),
         ((2, 2, 2 * count * states, LANES), f32),
+        ((2, 2 * count * states, LANES), bf16),
         ((2, eh, 2 * count * states + states * SUB, LANES), f32),
         ((2, eh, tall, LANES), f32),
         ((2, eh, tall, LANES), f32),
-        ((6, tall, LANES), f32),
+        ((eh, tall, LANES), f32),
+        ((eh, tall, LANES), f32),
+        ((eh, tall // 2, LANES), f32),
+        ((eh, tall, LANES), f32),
+        ((eh, tall // 2, LANES), f32),
+        ((2, count, LANES), f32),
         ((2, 2, eh, count, LANES), f32),
         ((tall, LANES), f32),
         ((tall, LANES), bf16),
@@ -1325,29 +1398,29 @@
         ((model, inner), f32),
         ((1, model), f32),
     ]
-    for lot in (early, late):
+    for lot in lots:
         chunk = (lot // rows, LANES)
         scratch += [((rows,) + chunk, f32), ((rows - 1,) + chunk, f32), ((cols,) + chunk, f32)]
-    feature, early_sum, late_sum = pl.pallas_call(
+    feature, *full = pl.pallas_call(
         functools.partial(fast_kernel, tile_rows, tile_cols, states, rank),
         out_shape=[
             jax.ShapeDtypeStruct((count, model), bf16),
-            jax.ShapeDtypeStruct((rows, early // rows, LANES), f32),
-            jax.ShapeDtypeStruct((rows, late // rows, LANES), f32),
-        ],
-        in_specs=[VMEM] * 11,
-        out_specs=[VMEM] * 3,
+        ]
+        + [jax.ShapeDtypeStruct((rows, lot // rows, LANES), f32) for lot in lots],
+        in_specs=[VMEM] * 13,
+        out_specs=[VMEM] * 5,
         scratch_shapes=[pltpu.VMEM(*s) for s in scratch]
         + [
-            pltpu.SemaphoreType.DMA((3, 2, 2, max(rows, cols))),
-            pltpu.SemaphoreType.DMA((2, 2, rows * cols)),
-            pltpu.SemaphoreType.DMA((2, 3, 2, max(rows, cols))),
+            pltpu.SemaphoreType.DMA((3, 2, 2)),
+            pltpu.SemaphoreType.DMA((2, 2)),
+            pltpu.SemaphoreType.DMA((4, 3, 2)),
         ],
         compiler_params=pltpu.CompilerParams(
-            vmem_limit_bytes=BIG, collective_id=1, has_side_effects=True
+            vmem_limit_bytes=BIG + 3 * 1024 * 1024, collective_id=1, has_side_effects=True
         ),
     )(
-        embedded, cotangent.reshape(count, model), norm_gain[None], in_weight, scan_weight.T,
+        features.reshape(count, model), classes, table, cotangent.reshape(count, model),
+        norm_gain[None], in_weight, scan_weight.T,
         step_weight, step_bias, decay_log, skip_gain, output_gain[None], output_weight,
     )
     shapes = [
@@ -1365,9 +1438,9 @@
     feature_grad, *grads = pl.pallas_call(
         functools.partial(unpack_kernel, states, rank, grad_scale),
         out_shape=[jax.ShapeDtypeStruct(*s) for s in shapes],
-        in_specs=[VMEM] * 3,
+        in_specs=[VMEM] * 5,
         out_specs=[VMEM] * 10,
-    )(feature, early_sum.reshape(early, LANES), late_sum.reshape(late, LANES))
+    )(feature, *[x.reshape(lot, LANES) for x, lot in zip(full, lots)])
     feature_grad = feature_grad.reshape(tile_rows, tile_cols, model)
     grads[1] = grads[1].T
     grads[6], grads[7] = grads[6][0], grads[7][0]
@@ -1380,7 +1453,7 @@
     rank, states, inner = args[7].shape[1], args[9].shape[1], args[12].shape[0]
     fits = (
         tile_rows == 4 * cols and tile_cols == 2 * rows and model == LANES and inner == 2 * LANES
-        and states == 2 * SUB and rank == SUB
+        and states == 2 * SUB and rank == SUB and args[3].shape[0] <= LANES
     )
     return (fast if fits else general)(*args)
 

time: 82.9 us -> 66.7 us (0.80)
  Pallas kernels: 79.6 us -> 65.8 us
  matrix products: 1.77 us -> 0 us
    pallas_call x1, Pallas kernels: 77.5 us -> 63.8 us  [fast(): pl.pallas_call(functools.partial(fast_kernel, tile_rows, tile_cols, state...]
    dot_general x1 -> x0, matrix products: 1.77 us -> none  [embed(): lookup = jnp.einsum('hwk,kd->hwd', onehot, table, precision=HIGHEST)]
where the time goes in v2:
time: 66.7 us; the launch traced here: 66.5 us
  Pallas kernels  65.8 us (99%)
    pallas_call x1, Pallas kernels, fast(): pl.pallas_call(functools.partial(fast_kernel, tile_rows, tile_cols, state...  63.8 us
    pallas_call x1, Pallas kernels, fast(): pl.pallas_call(functools.partial(unpack_kernel, states, rank, grad_scale)...  2.06 us

profile of v2, /device:TPU:0, one launch (start us, length us, event | category | flops | bytes accessed | tf_op | source)
XLA Modules:
  0.0 66.5 jit_solution(14078339621461707090)
XLA Ops:
  0.6 63.8 %shard_map.204 = (bf16[256,128]{1,0:T(8,128)(2,1)}, f32[8,72,128]{2,1,0:T(8,128)}, f32[8,40,128]{2,1,0:T(8,128)}, f32[8,40,128]{2,1,0:T(8,128)}, f32[8,40,128]{2,1,0:T(8,128)}) custom-call(bf16[256,128]{1,0:T(8,128)(2,1)} %bitcast.18, s32[16,16]{1,0:T(8,128)} %classes_ref.1, f32[16,128]{1,0:T(8,128)} %table_ref.1, bf16[256,128]{1,0:T(8,128)(2,1)} %bitcast.19, ...), custom_call_target="tpu_custom_call" | custom-call | tf_op jit(solution)/shard_map/pallas_call | solution.py:1404
  64.4 2.1 %shard_map.205 = (bf16[256,128]{1,0:T(8,128)(2,1)}, f32[128,512]{1,0:T(8,128)}, f32[160,256]{1,0:T(8,128)}, f32[4,8,256]{2,1,0:T(8,128)}, f32[4,256]{1,0:T(4,128...) custom-call(bf16[256,128]{1,0:T(8,128)(2,1)} %get-tuple-element.25.f, ...), custom_call_target="tpu_custom_call" | custom-call | tf_op jit(solution)/shard_map/pallas_call | solution.py:1438

commit v3 on v2

--- a/solution.py
+++ b/solution.py
@@ -613,7 +613,7 @@
     pair = (rank + states + group) * 2 * eh + -(-3 * eh // SUB) * SUB
     gated = SUB + inner * model_width // LANES + model_width * eh
     per = SUB * rows
-    return tuple(-(-n // per) * per for n in (gated, pair, pair, model_width * eh + SUB))
+    return tuple(-(-n // per) * per for n in (gated, pair, pair, model_width * eh))
 
 
 def fast_kernel(
@@ -624,7 +624,7 @@
     home, emb_s0, emb_s1, emb_r0, emb_r1, cot_s0, cot_s1, cot_r0, cot_r1,
     back_s0, back_s1, back_r0, back_r1, y_s0, y_s1, y_r0, y_r1,
     spread0, spread1, wpk, swp, cmat, rate_s, normed_s, mixed_s, value_s, proj_s, tok, slope,
-    wide, flows, hist, pace_t, drive_t, g_t, dd_a, dd_b, dp_a, dp_b, bufs, bufs_tok, probe_t, lhs, dval, dr_s, in_acc, norm_acc,
+    wide, flows, hist, pace_t, drive_t, g_t, dd_t, dp_t, bufs, bufs_tok, probe_t, lhs, dval, dr_s, in_acc,
     mine0, from0, side0, mine1, from1, side1, mine2, from2, side2, mine3, from3, side3,
     sems, ysems, sumsems,
 ):
@@ -657,6 +657,9 @@
     def tile(b):
         return pl.ds(pl.multiple_of(b * SUB, SUB), SUB)
 
+    def step_tile(p, b):
+        return tile(b + (length[0] if p else 0))
+
     def tile2(b):
         return pl.ds(pl.multiple_of(b * 2 * SUB, 2 * SUB), 2 * SUB)
 
@@ -751,14 +754,16 @@
     y_s, y_r = (y_s0, y_s1), (y_r0, y_r1)
     spreads = (spread0, spread1)
     pending = []
-    half_n = SUB
-    dd_t, dp_t = (dd_a, dd_b), (dp_a, dp_b)
+    half_n, few_n = SUB, SUB // 2
     y_t = dd_t
 
-    def added(refs, p, h, at):
-        total = refs[0][h, at, :]
-        for g in range(1, per_n[p] // half_n):
-            total = total + refs[g][h, at, :]
+    def group_tile(p, g, t):
+        return tile(g * length[p] + t)
+
+    def added(ref, p, h, b, groups):
+        total = ref[h, group_tile(p, 0, b), :]
+        for g in range(1, groups):
+            total = total + ref[h, group_tile(p, g, b), :]
         return total
 
     token = lax.broadcasted_iota(jnp.int32, (count, tile_rows), 0)
@@ -852,9 +857,9 @@
             x0, x1 = first(tile(b)), second(tile(mirror))
             if p == 0:
                 z = jnp.where(even, x1, x0)
-                store(tile(2 * b), jnp.where(even, x0, x1))
+                store(2 * b, jnp.where(even, x0, x1))
                 store(
-                    tile(2 * b + 1),
+                    2 * b + 1,
                     jnp.where(even, pltpu.roll(z, SUB - 1, 0), pltpu.roll(z, 1, 0)),
                 )
             else:
@@ -862,10 +867,10 @@
                 v = pltpu.roll(u, 4, 0)
                 u2 = pltpu.roll(jnp.where(pos_even, x1, x0), 2, 0)
                 v2 = pltpu.roll(u2, 4, 0)
-                store(tile(4 * b), jnp.where(pos_edge, u, v))
-                store(tile(4 * b + 1), jnp.where(low_half, v2, u2))
-                store(tile(4 * b + 2), jnp.where(pos_edge, v, u))
-                store(tile(4 * b + 3), jnp.where(low_half, u2, v2))
+                store(4 * b, jnp.where(pos_edge, u, v))
+                store(4 * b + 1, jnp.where(low_half, v2, u2))
+                store(4 * b + 2, jnp.where(pos_edge, v, u))
+                store(4 * b + 3, jnp.where(low_half, u2, v2))
 
         lax.fori_loop(0, blocks, one, 0, unroll=max(2, 4 // len(moves)))
 
@@ -878,13 +883,13 @@
         def one_of(b, load, store):
             mirror = blocks - 1 - b
             if p == 0:
-                s0, s1 = load(tile(2 * b)), load(tile(2 * b + 1))
+                s0, s1 = load(2 * b), load(2 * b + 1)
                 store(0, tile(b), jnp.where(even, s0, pltpu.roll(s1, 1, 0)))
                 store(1, tile(mirror), jnp.where(even, pltpu.roll(s1, SUB - 1, 0), s0))
             else:
                 a = []
                 for i in range(4):
-                    s = load(tile(4 * b + i))
+                    s = load(4 * b + i)
                     s = s + pltpu.roll(s, 4, 0)
                     a.append(pltpu.roll(s, 2, 0) if i % 2 else s)
                 store(
@@ -898,11 +903,14 @@
 
         lax.fori_loop(0, blocks, one, 0, unroll=max(2, 4 // len(moves)))
 
-    def put_at(ref, at, x):
-        ref[at, :] = x
-
-    def put_probe(at, x):
-        probe_t[at, :] = x
+    def put_step(ref, p, b, x):
+        ref[step_tile(p, b), :] = x
+
+    def put_at(ref, b, x):
+        ref[tile(b), :] = x
+
+    def put_probe(b, x):
+        probe_t[tile(b), :] = x
 
     def prologue(p):
         embedded = emb_r[p][...].reshape(count, model)
@@ -925,22 +933,34 @@
             bufs_tok[0, 0, h] = value32[:, part(h)]
             moves.append(
                 (lambda at, h=h: tok[p, 0, h, at, :], lambda at, h=h: tok[p, 1, h, at, :],
-                 functools.partial(put_at, pace_t.at[p, h]))
+                 functools.partial(put_step, pace_t.at[h], p))
             )
             moves.append(
                 (lambda at, h=h: tok[p, 0, h, at, :] * bufs_tok[0, 0, h, at, :],
                  lambda at, h=h: tok[p, 1, h, at, :] * bufs_tok[0, 0, h, at, :],
-                 functools.partial(put_at, drive_t.at[p, h]))
+                 functools.partial(put_step, drive_t.at[h], p))
             )
         to_scan(p, *moves)
         size_of = tall[p]
         x = jnp.where(keep_lanes(p, size_of), probe_t[:size_of, :], 0.0)
         high = x.astype(bf16).astype(f32)
         lhs[:size_of, :] = (high + pltpu.roll(x - high, 2 * states, 1)).astype(bf16)
+        if copies_m[p] > 1:
+            row = lax.broadcasted_iota(jnp.int32, (size_of, LANES), 0)
+            x = jnp.where(lax.rem(row, SUB) < 4, x, pltpu.roll(x, LANES - per_n[p], 1))
+        probe_t[:size_of, :] = x
         chunk = count
         for q in range(per_n[p]):
             w, n1 = 2 * q // per_n[p], 2 * q % per_n[p]
             for s in range(size_of // chunk):
+                if q % 3 == 2:
+                    for j in range(2):
+                        at = (n1 + j) * size_of + s * chunk
+                        col = w * states + n1 + j
+                        wide[p, w, at : at + chunk, :] = jnp.broadcast_to(
+                            probe_t[s * chunk : (s + 1) * chunk, col : col + 1], (chunk, LANES)
+                        )
+                    continue
                 out = dot(
                     lhs[s * chunk : (s + 1) * chunk, :],
                     spreads[p][:, 2 * q * LANES : 2 * (q + 1) * LANES],
@@ -965,12 +985,11 @@
                 hist[p, h, n * stride : n * stride + SUB, :] = zero
         for g in range(per_n[p] // half_n):
             ns = range(g * half_n, (g + 1) * half_n)
-            rates = [[rate_s[p, h, n * SUB : (n + 1) * SUB, :] for h in range(eh)] for n in ns]
-
-            def step(t, carry, g=g, ns=ns, rates=rates):
+
+            def step(t, carry, g=g, ns=ns):
                 at = tile(t)
-                pace = [pace_t[p, h, at, :] for h in range(eh)]
-                drive = [drive_t[p, h, at, :] for h in range(eh)]
+                pace = [pace_t[h, step_tile(p, t), :] for h in range(eh)]
+                drive = [drive_t[h, step_tile(p, t), :] for h in range(eh)]
                 y = [None] * eh
                 new = []
                 for i, n in enumerate(ns):
@@ -978,24 +997,24 @@
                     slot = tile(n * (stride // SUB) + t + 1)
                     source, probe = wide[p, 0, row, :], wide[p, 1, row, :]
                     for h in range(eh):
-                        a = jnp.exp2(pace[h] * rates[i][h])
+                        a = jnp.exp2(pace[h] * rate_s[p, h, n * SUB : (n + 1) * SUB, :])
                         state = a * carry[i * eh + h] + source * drive[h]
                         hist[p, h, slot, :] = state
                         new.append(state)
                         term = probe * state
                         y[h] = term if y[h] is None else y[h] + term
                 for h in range(eh):
-                    y_t[g][h, at, :] = y[h]
+                    y_t[h, group_tile(p, g, t), :] = y[h]
                 return tuple(new)
 
-            lax.fori_loop(0, length[p], step, (zero,) * (half_n * eh), unroll=2)
+            lax.fori_loop(0, length[p], step, (zero,) * (half_n * eh), unroll=8)
         moves = []
         for h in range(eh):
 
             def put_y(k, at, x, h=h):
                 bufs_tok[k, 0, h, at, :] = x
 
-            moves.append((lambda at, h=h: added(y_t, p, h, at), put_y))
+            moves.append((lambda b, h=h: added(y_t, p, h, b, per_n[p] // half_n), put_y))
         from_scan(p, *moves)
         for h in range(eh):
             y_s[p][:, :, part(h)] = (bufs_tok[0, 0, h] + bufs_tok[1, 0, h]).reshape(blocks, SUB, LANES)
@@ -1098,14 +1117,14 @@
 
     def backward(p):
         high, stride = tall[p], tall[p] + SUB
-        for g in range(per_n[p] // half_n):
-            ns = range(g * half_n, (g + 1) * half_n)
+        for g in range(per_n[p] // few_n):
+            ns = range(g * few_n, (g + 1) * few_n)
 
             def step(i, carry, g=g, ns=ns):
                 grads, rates, t = carry
                 at = tile(t)
-                pace = [pace_t[p, h, at, :] for h in range(eh)]
-                drive = [drive_t[p, h, at, :] for h in range(eh)]
+                pace = [pace_t[h, step_tile(p, t), :] for h in range(eh)]
+                drive = [drive_t[h, step_tile(p, t), :] for h in range(eh)]
                 gs = [g_t[h, at, :] for h in range(eh)]
                 dd, dp = [None] * eh, [None] * eh
                 new, new_rates = [], []
@@ -1139,13 +1158,13 @@
                         both = jnp.concatenate([kept[w], x], axis=0)
                         flows[w, place, :] = both.astype(bf16)
                 for h in range(eh):
-                    dd_t[g][h, at, :] = dd[h]
-                    dp_t[g][h, at, :] = dp[h]
+                    dd_t[h, group_tile(p, g, t), :] = dd[h]
+                    dp_t[h, group_tile(p, g, t), :] = dp[h]
                 return tuple(new), tuple(new_rates), t - 1
 
-            chains = (zero,) * (half_n * eh)
+            chains = (zero,) * (few_n * eh)
             unused, rates, end = lax.fori_loop(
-                0, length[p], step, (chains, chains, jnp.int32(length[p] - 1)), unroll=2
+                0, length[p], step, (chains, chains, jnp.int32(length[p] - 1)), unroll=4
             )
             for i, n in enumerate(ns):
                 for h in range(eh):
@@ -1181,7 +1200,7 @@
         def put_flow(k, at, x):
             bufs[k, at, :] = x
 
-        moves = [(lambda at: probe_t[at, :], put_flow)]
+        moves = [(lambda b: probe_t[tile(b), :], put_flow)]
         value16 = value_s[p]
         value = value16.astype(f32)
         d_total = dval[p]
@@ -1195,7 +1214,9 @@
                 def put_tok(k, at, x, which=which, h=h):
                     bufs_tok[k, which, h, at, :] = x
 
-                moves.append((lambda at, source=source, h=h: added(source, p, h, at), put_tok))
+                moves.append(
+                    (lambda b, source=source, h=h: added(source, p, h, b, per_n[p] // few_n), put_tok)
+                )
         from_scan(p, *moves)
         for k in range(2):
             d = 2 * p + k
@@ -1226,28 +1247,23 @@
                     put(lot, acc)
         put(lot, pad_rows(*small))
         steps = [sum_scatter(lot)]
-        if p == 1:
-            between()
         d_val = (dv * silu_slope(mixed_s[p, :, :inner])).astype(bf16)
         grad = cross(normed_s[p], d_val)
         if p == 0:
             in_acc[...] = grad
-            d_mixed = jnp.concatenate([d_val, gate16], axis=1)
-            d_normed = back(d_mixed, in_weight_ref[...])
-        else:
-            put_wide(3, in_acc[...] + grad)
-            d_normed = back(d_val, in_weight_ref[:, :inner])
-        unused, pull = jax.vjp(layer_norm, emb_r[p][...].reshape(count, model), norm_gain_ref[...])
-        d_embedded, norm_grad = pull(d_normed)
-        if p == 0:
-            norm_acc[...] = norm_grad
-        else:
-            put(3, pad_rows(norm_acc[...] + norm_grad))
-            steps.append(sum_scatter(3))
-        back_s[p][...] = d_embedded.reshape(back_s[p].shape)
+            return steps[0], jnp.concatenate([d_val, gate16], axis=1)
+        put_wide(3, in_acc[...] + grad)
+        return steps[0], sum_scatter(3), d_val
+
+    def go_home(p, d_mixed):
+        d_normed = back(d_mixed, in_weight_ref[:, : d_mixed.shape[1]])
+        unused, pull = jax.vjp(
+            lambda x: layer_norm(x, norm_gain_ref[...]), emb_r[p][...].reshape(count, model)
+        )
+        back_s[p][...] = pull(d_normed)[0].reshape(back_s[p].shape)
         out = exchange(2, p, back_s[p], back_r[p])
         pending.extend(out)
-        return [out] + steps
+        return out
 
     arrived(emb1)
     prologue(1)
@@ -1264,22 +1280,22 @@
     gate16 = gate(0)
     first = sum_scatter(0)
     backward(0)
+    second, d_mixed = finish_pair(0, gate16)
+    home0 = go_home(0, d_mixed)
     first = sum_across(0, first)
-    home0, second = finish_pair(0, gate16)
-    first = sum_gather(0, first)
     arrived(y0)
     arrived(cot1)
     gate(1)
     backward(1)
     flying = [sum_across(1, second)]
 
-    def between():
-        flying.append(sum_gather(1, flying[0]))
-
-    home1, third, fourth = finish_pair(1, None)
-    sent(pending[:-3])
-    del pending[:-3]
+    third, fourth, d_mixed = finish_pair(1, None)
+    home1 = go_home(1, d_mixed)
+    first = sum_gather(0, first)
     third = sum_across(2, third)
+    flying.append(sum_gather(1, flying[0]))
+    sent(pending[:-4])
+    del pending[:-4]
     home[...] = upstream_ref[...].astype(f32)
     arrived(home0)
     unpack(back_r0, bufs.at[0], 0)
@@ -1297,7 +1313,7 @@
 
 def unpack_kernel(
     states, rank, grad_scale,
-    feature_in, full0, full1, full2, full3,
+    feature_in, full0, full1, full2, full3, in_weight_ref, norm_gain_ref,
     feature_ref, in_grad_ref, scan_grad_ref, stepw_ref, stepb_ref, dr_ref, skip_grad_ref,
     norm_grad_ref, gain_grad_ref, out_grad_ref,
 ):
@@ -1342,7 +1358,14 @@
                 skip_grad_ref[d : d + 1, part(h)] = small[h : h + 1]
                 stepb_ref[d : d + 1, part(h)] = small[(k + 1) * eh + h : (k + 1) * eh + h + 1]
     take_wide(3, in_grad_ref, 0, model, inner)
-    norm_grad_ref[...] = take(3, SUB)[0:1]
+    weighed = in_grad_ref[...] * in_weight_ref[...].astype(jnp.float32)
+    norm_grad_ref[...] = (
+        lax.dot_general(
+            jnp.ones((SUB, weighed.shape[1]), jnp.float32), weighed, (((1,), (1,)), ((), ())),
+            precision=HIGHEST, preferred_element_type=jnp.float32,
+        )[0:1]
+        / norm_gain_ref[...]
+    )
 
 
 def fast(
@@ -1358,7 +1381,8 @@
     eh = inner // LANES
     grad_scale = float(count * rows * cols) ** (-0.5)
     f32, bf16 = jnp.float32, jnp.bfloat16
-    tall = max(SUB * count // (tile_rows // cols), SUB * count // (tile_cols // rows))
+    talls = (SUB * count // (tile_rows // cols), SUB * count // (tile_cols // rows))
+    tall, sum_tall = max(talls), sum(talls)
     blocks = count // SUB
     lots = lots_of(rows, inner, model, states, rank, group, eh)
     per_row = ((cols, count // cols, model), (rows, count // rows, model))
@@ -1382,13 +1406,11 @@
         ((2, 2, 2 * count * states, LANES), f32),
         ((2, 2 * count * states, LANES), bf16),
         ((2, eh, 2 * count * states + states * SUB, LANES), f32),
-        ((2, eh, tall, LANES), f32),
-        ((2, eh, tall, LANES), f32),
+        ((eh, sum_tall, LANES), f32),
+        ((eh, sum_tall, LANES), f32),
         ((eh, tall, LANES), f32),
-        ((eh, tall, LANES), f32),
-        ((eh, tall // 2, LANES), f32),
-        ((eh, tall, LANES), f32),
-        ((eh, tall // 2, LANES), f32),
+        ((eh, 2 * tall, LANES), f32),
+        ((eh, 2 * tall, LANES), f32),
         ((2, count, LANES), f32),
         ((2, 2, eh, count, LANES), f32),
         ((tall, LANES), f32),
@@ -1396,7 +1418,6 @@
         ((2, count, inner), f32),
         ((eh, states * SUB, LANES), f32),
         ((model, inner), f32),
-        ((1, model), f32),
     ]
     for lot in lots:
         chunk = (lot // rows, LANES)
@@ -1438,9 +1459,11 @@
     feature_grad, *grads = pl.pallas_call(
         functools.partial(unpack_kernel, states, rank, grad_scale),
         out_shape=[jax.ShapeDtypeStruct(*s) for s in shapes],
-        in_specs=[VMEM] * 5,
+        in_specs=[VMEM] * 7,
         out_specs=[VMEM] * 10,
-    )(feature, *[x.reshape(lot, LANES) for x, lot in zip(full, lots)])
+    )(
+        feature, *[x.reshape(lot, LANES) for x, lot in zip(full, lots)], in_weight, norm_gain[None]
+    )
     feature_grad = feature_grad.reshape(tile_rows, tile_cols, model)
     grads[1] = grads[1].T
     grads[6], grads[7] = grads[6][0], grads[7][0]

time: 66.7 us -> 63 us (0.945)
  Pallas kernels: 65.8 us -> 62.2 us
    pallas_call x1, Pallas kernels: 63.8 us -> 60 us  [fast(): pl.pallas_call(functools.partial(fast_kernel, tile_rows, tile_cols, state...]
where the time goes in v3:
time: 63 us; the launch traced here: 62.9 us
  Pallas kernels  62.2 us (99%)
  between operations  0.65 us (1%)
    pallas_call x1, Pallas kernels, fast(): pl.pallas_call(functools.partial(fast_kernel, tile_rows, tile_cols, state...  60 us
    pallas_call x1, Pallas kernels, fast(): pl.pallas_call(functools.partial(unpack_kernel, states, rank, grad_scale)...  2.18 us

profile of v3, /device:TPU:0, one launch (start us, length us, event | category | flops | bytes accessed | tf_op | source)
XLA Modules:
  0.0 62.9 jit_solution(3419890349953239933)
XLA Ops:
  0.6 60.0 %shard_map.204 = (bf16[256,128]{1,0:T(8,128)(2,1)}, f32[8,72,128]{2,1,0:T(8,128)}, f32[8,40,128]{2,1,0:T(8,128)}, f32[8,40,128]{2,1,0:T(8,128)}, f32[8,32,128]{2,1,0:T(8,128)}) custom-call(bf16[256,128]{1,0:T(8,128)(2,1)} %bitcast.18, s32[16,16]{1,0:T(8,128)} %classes_ref.1, f32[16,128]{1,0:T(8,128)} %table_ref.1, bf16[256,128]{1,0:T(8,128)(2,1)} %bitcast.19, ...), custom_call_target="tpu_custom_call" | custom-call | tf_op jit(solution)/shard_map/pallas_call | solution.py:1425
  60.7 2.2 %shard_map.205 = (bf16[256,128]{1,0:T(8,128)(2,1)}, f32[128,512]{1,0:T(8,128)}, f32[160,256]{1,0:T(8,128)}, f32[4,8,256]{2,1,0:T(8,128)}, f32[4,256]{1,0:T(4,128...) custom-call(bf16[256,128]{1,0:T(8,128)(2,1)} %get-tuple-element.25.f, ...), custom_call_target="tpu_custom_call" | custom-call | tf_op jit(solution)/shard_map/pallas_call | solution.py:1459

commit v4 on v3

--- a/solution.py
+++ b/solution.py
@@ -1115,9 +1115,11 @@
         full[me_r] = acc
         return spread(lot, 2, "row", lambda t: full.at[me_r], lambda m, d: full.at[m], full)
 
-    def backward(p):
+    def backward(p, hook=None):
         high, stride = tall[p], tall[p] + SUB
         for g in range(per_n[p] // few_n):
+            if hook is not None and g == 1:
+                hook()
             ns = range(g * few_n, (g + 1) * few_n)
 
             def step(i, carry, g=g, ns=ns):
@@ -1261,6 +1263,8 @@
             lambda x: layer_norm(x, norm_gain_ref[...]), emb_r[p][...].reshape(count, model)
         )
         back_s[p][...] = pull(d_normed)[0].reshape(back_s[p].shape)
+
+    def send_home(p):
         out = exchange(2, p, back_s[p], back_r[p])
         pending.extend(out)
         return out
@@ -1273,26 +1277,28 @@
     arrived(emb0)
     prologue(0)
     forward(0)
+    arrived(y1)
+    arrived(cot0)
     y0 = swap(0, y_s0, y_r1)
     pending += y0
-    arrived(y1)
-    arrived(cot0)
     gate16 = gate(0)
     first = sum_scatter(0)
     backward(0)
     second, d_mixed = finish_pair(0, gate16)
-    home0 = go_home(0, d_mixed)
+    go_home(0, d_mixed)
     first = sum_across(0, first)
+    home0 = send_home(0)
     arrived(y0)
     arrived(cot1)
     gate(1)
     backward(1)
+    first = sum_gather(0, first)
     flying = [sum_across(1, second)]
 
     third, fourth, d_mixed = finish_pair(1, None)
-    home1 = go_home(1, d_mixed)
-    first = sum_gather(0, first)
     third = sum_across(2, third)
+    go_home(1, d_mixed)
+    home1 = send_home(1)
     flying.append(sum_gather(1, flying[0]))
     sent(pending[:-4])
     del pending[:-4]

time: 63 us -> 60.8 us (0.965)
  Pallas kernels: 62.2 us -> 60 us
    pallas_call x1, Pallas kernels: 60 us -> 57.8 us  [fast(): pl.pallas_call(functools.partial(fast_kernel, tile_rows, tile_cols, state...]
where the time goes in v4:
time: 60.8 us; the launch traced here: 60.7 us
  Pallas kernels  60 us (99%)
  between operations  0.65 us (1%)
    pallas_call x1, Pallas kernels, fast(): pl.pallas_call(functools.partial(fast_kernel, tile_rows, tile_cols, state...  57.8 us
    pallas_call x1, Pallas kernels, fast(): pl.pallas_call(functools.partial(unpack_kernel, states, rank, grad_scale)...  2.18 us

profile of v4, /device:TPU:0, one launch (start us, length us, event | category | flops | bytes accessed | tf_op | source)
XLA Modules:
  0.0 60.7 jit_solution(16262458246716969231)
XLA Ops:
  0.6 57.8 %shard_map.204 = (bf16[256,128]{1,0:T(8,128)(2,1)}, f32[8,72,128]{2,1,0:T(8,128)}, f32[8,40,128]{2,1,0:T(8,128)}, f32[8,40,128]{2,1,0:T(8,128)}, f32[8,32,128]{2,1,0:T(8,128)}) custom-call(bf16[256,128]{1,0:T(8,128)(2,1)} %bitcast.18, s32[16,16]{1,0:T(8,128)} %classes_ref.1, f32[16,128]{1,0:T(8,128)} %table_ref.1, bf16[256,128]{1,0:T(8,128)(2,1)} %bitcast.19, ...), custom_call_target="tpu_custom_call" | custom-call | tf_op jit(solution)/shard_map/pallas_call | solution.py:1431
  58.5 2.2 %shard_map.205 = (bf16[256,128]{1,0:T(8,128)(2,1)}, f32[128,512]{1,0:T(8,128)}, f32[160,256]{1,0:T(8,128)}, f32[4,8,256]{2,1,0:T(8,128)}, f32[4,256]{1,0:T(4,128...) custom-call(bf16[256,128]{1,0:T(8,128)(2,1)} %get-tuple-element.25.f, ...), custom_call_target="tpu_custom_call" | custom-call | tf_op jit(solution)/shard_map/pallas_call | solution.py:1465

commit v5 on v4

--- a/solution.py
+++ b/solution.py
@@ -872,7 +872,7 @@
                 store(4 * b + 2, jnp.where(pos_edge, v, u))
                 store(4 * b + 3, jnp.where(low_half, u2, v2))
 
-        lax.fori_loop(0, blocks, one, 0, unroll=max(2, 4 // len(moves)))
+        lax.fori_loop(0, blocks, one, 0, unroll=4)
 
     def from_scan(p, *moves):
         def one(b, carry):
@@ -901,7 +901,7 @@
                     jnp.where(low_half, jnp.where(pos == 0, a[3], a[2]), jnp.where(pos == 2, a[1], a[0])),
                 )
 
-        lax.fori_loop(0, blocks, one, 0, unroll=max(2, 4 // len(moves)))
+        lax.fori_loop(0, blocks, one, 0, unroll=4)
 
     def put_step(ref, p, b, x):
         ref[step_tile(p, b), :] = x

time: 60.8 us -> 60.4 us (level)
  no operation moved by 1% of the time
where the time goes in v5:
time: 60.4 us; the launch traced here: 60.2 us
  Pallas kernels  59.6 us (99%)
  between operations  0.65 us (1%)
    pallas_call x1, Pallas kernels, fast(): pl.pallas_call(functools.partial(fast_kernel, tile_rows, tile_cols, state...  57.4 us
    pallas_call x1, Pallas kernels, fast(): pl.pallas_call(functools.partial(unpack_kernel, states, rank, grad_scale)...  2.18 us

profile of v5, /device:TPU:0, one launch (start us, length us, event | category | flops | bytes accessed | tf_op | source)
XLA Modules:
  0.0 60.2 jit_solution(9998507586067817003)
XLA Ops:
  0.6 57.4 %shard_map.204 = (bf16[256,128]{1,0:T(8,128)(2,1)}, f32[8,72,128]{2,1,0:T(8,128)}, f32[8,40,128]{2,1,0:T(8,128)}, f32[8,40,128]{2,1,0:T(8,128)}, f32[8,32,128]{2,1,0:T(8,128)}) custom-call(bf16[256,128]{1,0:T(8,128)(2,1)} %bitcast.18, s32[16,16]{1,0:T(8,128)} %classes_ref.1, f32[16,128]{1,0:T(8,128)} %table_ref.1, bf16[256,128]{1,0:T(8,128)(2,1)} %bitcast.19, ...), custom_call_target="tpu_custom_call" | custom-call | tf_op jit(solution)/shard_map/pallas_call | solution.py:1431
  58.0 2.2 %shard_map.205 = (bf16[256,128]{1,0:T(8,128)(2,1)}, f32[128,512]{1,0:T(8,128)}, f32[160,256]{1,0:T(8,128)}, f32[4,8,256]{2,1,0:T(8,128)}, f32[4,256]{1,0:T(4,128...) custom-call(bf16[256,128]{1,0:T(8,128)(2,1)} %get-tuple-element.25.f, ...), custom_call_target="tpu_custom_call" | custom-call | tf_op jit(solution)/shard_map/pallas_call | solution.py:1465
